TPU v7x, 256 devices: a whole 4x4x8 slice. The times are simulated.
256 devices in a mesh: beam: 8 (over y_hi, x), blk: 32 (over y_lo, z, core).
Axes of the slice: x: 4, y: 4 (y_hi: 2, y_lo: 2; y = y_hi * 2 + y_lo), z: 8, core: 2. Of those that a mesh axis runs over, the one named last changes fastest.
Arguments:
- hidden_in: bfloat16 [256, 4096], P('beam', 'blk'), may hold values from -250 to 250
- self_gain: bfloat16 [4096], P('blk'), may hold values from 0.099609375 to 1.8984375
- w_self: bfloat16 [4096, 3, 4096], P(None, None, 'blk'), may hold values from -0.09375 to 0.09375
- w_self_out: bfloat16 [4096, 4096], P('blk'), may hold values from -0.1875 to 0.1875
- cross_gain: bfloat16 [4096], P('blk'), may hold values from 0.099609375 to 1.8984375
- w_cross_q: bfloat16 [4096, 4096], P('blk'), may hold values from -0.09375 to 0.09375
- w_cross_out: bfloat16 [4096, 4096], P(None, 'blk'), may hold values from -0.09375 to 0.09375
- cache_kv: bfloat16 [256, 128, 64, 128], P('beam', None, 'blk'), may hold values from -1000 to 1000
- memory_kv: bfloat16 [8192, 8192], P('blk'), may hold values from -1000 to 1000
- parents: int32 [256], replicated, may hold values from 0 to 255
- prefix_len: int32 [256], replicated, may hold values from 65 to 128, as said below
Outputs:
- result: bfloat16 [256, 4096], P('beam', 'blk')
Inputs may be any that keep to these rules, and one draw needn't show every extreme that they name: New hypothesis i continues the cache of old hypothesis parents[i]. Cache positions below prefix_len[i] hold decoded tokens of new hypothesis i.
All inputs are finite; a program needn't handle non-finite values.
Results may differ from a plain program's by a relative error of at most 0.013.
Values may be sent and summed in bfloat16 or wider, within the bound.
A program may use at most 128 MiB of HBM per device.

v0:
```python
import jax
import jax.numpy as jnp
from jax import lax
from jax.sharding import PartitionSpec as P

D = 4096
HEADS = 64
HEAD_DIM = 64


NEG = -1e30
EPS = 1e-06


def joined(part, axis, combine):
    gathered = jax.tree.map(lambda a: lax.all_gather(a, axis), part)

    def take(source):
        return jax.tree.map(lambda a: lax.dynamic_index_in_dim(a, source, 0, False), gathered)

    return lax.fori_loop(
        1, lax.axis_size(axis), lambda source, state: combine(state, take(source)), take(0)
    )


def soft_parts(scores, visible):
    masked = jnp.where(visible, scores, NEG)
    maxima = jnp.max(masked, axis=-1)
    weights = jnp.where(visible, jnp.exp(masked - maxima[..., None]), 0.0)
    rounded = weights.astype(jnp.bfloat16)
    totals = jnp.sum(rounded.astype(jnp.float32), axis=-1)
    return (maxima, totals, rounded)


def combine(earlier, later):
    highest = jnp.maximum(earlier[0], later[0])
    first_weight = jnp.exp(earlier[0] - highest)
    second_weight = jnp.exp(later[0] - highest)
    return (
        highest,
        earlier[1] * first_weight + later[1] * second_weight,
        earlier[2] * first_weight[..., None] + later[2] * second_weight[..., None],
    )


def finish_plain(totals, weighted):
    attended = weighted / totals[..., None]
    return attended.reshape(attended.shape[0], -1).astype(jnp.bfloat16)


def finish_self(maxima, totals, weighted, own_score, own_value):
    highest = jnp.maximum(maxima, own_score)
    factor = jnp.exp(maxima - highest)
    own_weight = jnp.exp(own_score - highest)
    numerator = weighted * factor[..., None] + own_weight[..., None] * own_value
    denominator = totals * factor + own_weight
    attended = numerator / denominator[..., None]
    return attended.reshape(attended.shape[0], -1).astype(jnp.bfloat16)


def merge_memory(partials):
    merged = joined(partials, "blk", combine)
    return finish_plain(merged[1], merged[2])


def cache_stats(query_heads, cache_rows, visible, score_scale):
    head_dim = query_heads.shape[2]
    key_heads = cache_rows[..., :head_dim]
    value_heads = cache_rows[..., head_dim:]
    scores = (
        jnp.einsum("ihd,iphd->ihp", query_heads, key_heads, preferred_element_type=jnp.float32)
        * score_scale
    )
    maxima, totals, rounded = soft_parts(scores, visible[:, None, :])
    weighted = jnp.einsum("ihp,iphd->ihd", rounded, value_heads, preferred_element_type=jnp.float32)
    return (maxima, totals, weighted)


def body(
    hidden_in,
    self_gain,
    w_self,
    w_self_out,
    cross_gain,
    w_cross_q,
    w_cross_out,
    cache_kv,
    memory_kv,
    parents,
    prefix_len,
):
    row_count = hidden_in.shape[0]
    head_count = cache_kv.shape[2]
    head_dim = cache_kv.shape[3] // 2
    local_width = head_count * head_dim
    score_scale = head_dim ** (-0.5)
    full_rows, full_gain = (
        lax.all_gather(hidden_in, "blk", axis=1, tiled=True),
        lax.all_gather(self_gain, "blk", axis=0, tiled=True),
    )
    wide_rows = full_rows.astype(jnp.float32)
    self_mean = jnp.mean(wide_rows * wide_rows, axis=1)
    scaled = (wide_rows * full_gain.astype(jnp.float32)).astype(jnp.bfloat16)
    flat_weight = w_self.reshape(w_self.shape[0], 3 * local_width)
    projected = (
        jnp.dot(scaled, flat_weight, preferred_element_type=jnp.float32)
        * lax.rsqrt(self_mean + EPS)[:, None]
    ).astype(jnp.bfloat16)
    queries = projected[:, :local_width]
    query_heads = queries.reshape(row_count, head_count, head_dim)
    own_keys = (
        projected[:, local_width : 2 * local_width]
        .reshape(row_count, head_count, head_dim)
        .astype(jnp.float32)
    )
    own_value = (
        projected[:, 2 * local_width :].reshape(row_count, head_count, head_dim).astype(jnp.float32)
    )
    own_score = jnp.sum(query_heads.astype(jnp.float32) * own_keys, axis=-1) * score_scale
    cache_len = cache_kv.shape[1]
    positions = jnp.arange(cache_len, dtype=jnp.int32)
    first_mine = lax.axis_index("beam") * row_count
    my_parents = lax.dynamic_slice_in_dim(parents, first_mine, row_count, 0)
    my_lengths = lax.dynamic_slice_in_dim(prefix_len, first_mine, row_count, 0)
    visible = positions[None, :] < my_lengths[:, None]
    shard_rows = lax.all_gather(cache_kv, "beam", axis=0, tiled=True)
    held_rows = shard_rows.shape[0]
    inside = (my_parents >= 0) & (my_parents < held_rows)
    chosen = jnp.take(shard_rows, jnp.clip(my_parents, 0, held_rows - 1), axis=0)
    reordered = jnp.where(inside[:, None, None, None], chosen, jnp.zeros_like(cache_kv))
    cache_max, cache_total, cache_sum = cache_stats(query_heads, reordered, visible, score_scale)
    self_attended = finish_self(cache_max, cache_total, cache_sum, own_score, own_value)
    head_terms = jnp.dot(self_attended, w_self_out, preferred_element_type=jnp.float32)
    mixed = lax.psum_scatter(head_terms, "blk", scatter_dimension=1, tiled=True)
    middle = (hidden_in.astype(jnp.float32) + mixed).astype(jnp.bfloat16)
    middle_wide = middle.astype(jnp.float32)
    cross_squares = jnp.sum(middle_wide * middle_wide, axis=1)
    cross_scaled = (middle_wide * cross_gain.astype(jnp.float32)).astype(jnp.bfloat16)
    cross_partial = jnp.dot(cross_scaled, w_cross_q, preferred_element_type=jnp.float32)
    cross_squares, cross_partial = lax.psum((cross_squares, cross_partial), "blk")
    cross_heads = (
        (cross_partial * lax.rsqrt(cross_squares / D + EPS)[:, None])
        .astype(jnp.bfloat16)
        .reshape(row_count, HEADS, HEAD_DIM)
    )
    memory_count = memory_kv.shape[0]
    head_width = HEADS * HEAD_DIM
    memory_keys = memory_kv[:, :head_width].reshape(memory_count, HEADS, HEAD_DIM)
    memory_values = memory_kv[:, head_width:].reshape(memory_count, HEADS, HEAD_DIM)
    memory_scores = (
        jnp.einsum("ihd,phd->ihp", cross_heads, memory_keys, preferred_element_type=jnp.float32)
        * score_scale
    )
    maxima, totals, rounded = soft_parts(
        memory_scores, jnp.ones((1, 1, memory_count), dtype=jnp.bool_)
    )
    weighted = jnp.einsum(
        "ihp,phd->ihd", rounded, memory_values, preferred_element_type=jnp.float32
    )
    crossed = merge_memory((maxima, totals, weighted))
    return (middle_wide + jnp.dot(crossed, w_cross_out, preferred_element_type=jnp.float32)).astype(
        jnp.bfloat16
    )


def solution(mesh):
    return jax.shard_map(
        body,
        mesh=mesh,
        in_specs=(
            P("beam", "blk"),
            P("blk"),
            P(None, None, "blk"),
            P("blk", None),
            P("blk"),
            P("blk", None),
            P(None, "blk"),
            P("beam", None, "blk", None),
            P("blk", None),
            P(),
            P(),
        ),
        out_specs=P("beam", "blk"),
        check_vma=False,
    )
```

profile of v0, /device:TPU:1, one launch (start us, length us, event | category | flops | bytes accessed | tf_op | source)
XLA Modules:
  0.0 869.2 jit_solution(4391486161282118503)
XLA Ops:
  6.5 3.6 copy.69
  10.8 38.6 %all-gather.3 = bf16[32,1,128]{2,1,0:T(2,128)(2,1)S(1)} all-gather(bf16[1,1,128]{2,1,0:T(2,128)(2,1)S(1)} %bitcast.72), channel_id=1, replica_groups=mesh['beam'=8,'blk'=32] {'blk'}, dimensions={0}, use_global_device_ids=true | all-gather | bytes 8448 | tf_op jit(solution)/shard_map/all_gather | solution.py:99
  49.4 4.7 copy.68
  54.1 31.5 %all_gather.27 = bf16[32,4096]{1,0:T(8,128)(2,1)S(1)} all-gather(bf16[32,128]{1,0:T(8,128)(2,1)S(1)} %copy-done.4), channel_id=1, replica_groups=mesh['beam'=8,'blk'=32] {'blk'}, dimensions={1}, use_global_device_ids=true | all-gather | bytes 270336 | tf_op jit(solution)/shard_map/all_gather | solution.py:98
  85.8 2.9 fusion.10
  89.5 114.6 %all-gather.7.cloned.1.call-done = bf16[256,128,2,128]{3,1,2,0:T(8,128)(2,1)} async-done(((bf16[32,128,2,128]{3,1,2,0:T(8,128)(2,1)}), bf16[256,128,2,128]{3,1,2,0:T(8,128)(2,1)}) %all-gather.7.cloned.1.call-update) | async-done | bytes 16777232 | tf_op jit(solution)/shard_map/all_gather | solution.py:126
  204.2 6.7 gather_fusion
  215.2 112.1 %reduce-scatter.2.cloned.1.call-done = f32[32,128]{1,0:T(8,128)} async-done(((f32[32,4096]{1,0:T(8,128)}), f32[32,128]{1,0:T(8,128)}) %reduce-scatter.2.cloned.1.call-update) | async-done | bytes 16400 | tf_op jit(solution)/shard_map/reduce_scatter | solution.py:134
  329.3 3.9 fusion.35
  333.2 4.1 copy.78
  337.3 2.4 copy.74
  339.7 56.7 %psum.15 = f32[32]{0:T(128)S(1)} all-reduce(f32[32]{0:T(128)S(1)} %get-tuple-element.251), channel_id=1, replica_groups=mesh['beam'=8,'blk'=32] {'blk'}, use_global_device_ids=true, to_apply=%region_7.8 | all-reduce | flops 32 | bytes 256 | tf_op jit(solution)/shard_map/psum | solution.py:140
  396.4 158.6 %all-reduce.2.cloned.1.call-done = f32[32,4096]{1,0:T(8,128)} async-done(((f32[32,4096]{1,0:T(8,128)}), f32[32,4096]{1,0:T(8,128)}) %all-reduce.2.cloned.1.call-update) | async-done | bytes 524304 | tf_op jit(solution)/shard_map/psum | solution.py:140
  556.7 2.4 bitcast_reduce_fusion
  559.1 1.8 convolution_bitcast_fusion
  561.8 35.6 %all-gather.1 = f32[1024,64]{1,0:T(8,128)} all-gather(f32[32,64]{1,0:T(8,128)S(1)} %copy.77), channel_id=3, replica_groups=mesh['beam'=8,'blk'=32] {'blk'}, dimensions={0}, use_global_device_ids=true | all-gather | bytes 270336 | tf_op jit(solution)/shard_map/all_gather | solution.py:16
  598.1 38.1 %all-gather = f32[1024,64]{1,0:T(8,128)} all-gather(f32[32,64]{1,0:T(8,128)S(1)} %copy.76), channel_id=2, replica_groups=mesh['beam'=8,'blk'=32] {'blk'}, dimensions={0}, use_global_device_ids=true | all-gather | bytes 270336 | tf_op jit(solution)/shard_map/all_gather | solution.py:16
  636.9 111.9 %all-gather.9.cloned.1.call-done = f32[1024,64,64]{2,0,1:T(8,128)} async-done(((f32[32,64,64]{2,0,1:T(8,128)}), f32[1024,64,64]{2,0,1:T(8,128)}) %all-gather.9.cloned.1.call-update) | async-done | bytes 16777232 | tf_op jit(solution)/shard_map/all_gather | solution.py:16
  750.6 109.1 %while.19 = (s32[]{:T(128)}, f32[32,64]{1,0:T(8,128)S(1)}, f32[32,64]{1,0:T(8,128)S(1)}, f32[32,64,64]{2,1,0:T(8,128)S(1)}, f32[32,32,64]{2,1,0:T(8,128)}, /*ind...) while((s32[]{:T(128)}, f32[32,64]{1,0:T(8,128)S(1)}, ...), condition=%wide.region_11.12_spmd, body=%wide.region_10.11_spmd.sunk | while | flops 405509 | bytes 2703503 | solution.py:21
  752.7 1.4 fusion.49
  756.2 1.4 fusion.49
  763.2 1.4 fusion.49
  766.8 1.4 fusion.49
  773.8 1.4 fusion.49
  777.3 1.4 fusion.49
  784.4 1.4 fusion.49
  787.9 1.4 fusion.49
  794.9 1.4 fusion.49
  798.5 1.4 fusion.49
  805.5 1.4 fusion.49
  809.0 1.4 fusion.49
  860.6 2.1 fusion.11
  (149 shorter events, 105.6 us)
Async XLA Ops:
  6.5 207.5 %copy-start = (bf16[128,4096]{1,0:T(8,128)(2,1)S(1)}, bf16[128,4096]{1,0:T(8,128)(2,1)}, u32[]{:S(2)}) copy-start(bf16[128,4096]{1,0:T(8,128)(2,1)} %param.16) | copy-start | bytes 3145732
  6.5 197.6 %all-gather.7.cloned.1.call-start = ((), (), s32[]{:S(2)}) async-start(), calls=%async_computation.1 | async-start | bytes 18874368 | tf_op jit(solution)/shard_map/all_gather | solution.py:126
  10.1 0.7 copy-start.5
  10.2 317.1 %reduce-scatter.2.cloned.1.call-start = ((), (), s32[]{:S(2)}) async-start(), calls=%async_computation.2 | async-start | bytes 540672 | tf_op jit(solution)/shard_map/reduce_scatter | solution.py:134
  49.4 4.7 copy-start.4
  54.1 35.2 %copy-start.7 = (s32[256]{0:T(256)S(1)}, s32[256]{0:T(256)}, u32[]{:S(2)}) copy-start(s32[256]{0:T(256)} %param.23) | copy-start | bytes 3076
  54.1 35.3 %copy-start.6 = (s32[256]{0:T(256)S(1)}, s32[256]{0:T(256)}, u32[]{:S(2)}) copy-start(s32[256]{0:T(256)} %param.22) | copy-start | bytes 3076
  212.7 2.5 copy-start.8
  212.7 115.4 %copy-start.3 = (bf16[128,4096]{1,0:T(8,128)(2,1)S(1)}, bf16[128,4096]{1,0:T(8,128)(2,1)}, u32[]{:S(2)}) copy-start(bf16[128,4096]{1,0:T(8,128)(2,1)} %param.18) | copy-start | bytes 3145732
  215.1 339.9 %all-reduce.2.cloned.1.call-start = ((), (), s32[]{:S(2)}) async-start(), calls=%async_computation.3 | async-start | bytes 1048576 | tf_op jit(solution)/shard_map/psum | solution.py:140
  329.2 419.5 %all-gather.9.cloned.1.call-start = ((), (), s32[]{:S(2)}) async-start(), calls=%async_computation.4 | async-start | bytes 34603008 | tf_op jit(solution)/shard_map/all_gather | solution.py:16
  556.7 2.4 copy-start.2
  748.8 1.2 slice-start
  859.7 2.9 copy-start.1
Sparse Core Ops, SparseCore 0:
  10.3 193.8 all-gather.6
  215.2 111.9 reduce-scatter.1
  329.9 225.1 all-reduce.1
  561.0 187.6 all-gather.8
where the time goes:
time: 876 us; the launch traced here: 869 us
  waiting for transfers between devices  497 us (57%)
  blocking collectives  200 us (23%)
  local copies, waits for them, and re-layouts  72 us (8%)
  other arithmetic  71.9 us (8%)
  matrix products  13.3 us (2%)
  between operations  13.3 us (2%)
    psum x1, waiting for transfers between devices, body(): lax.psum((cross_squares, cross_partial), 'blk')  159 us
    all_gather x1, waiting for transfers between devices, body(): shard_rows = lax.all_gather(cache_kv, 'beam', axis=0, tiled=True)  115 us
    reduce_scatter x1, waiting for transfers between devices, body(): mixed = lax.psum_scatter(head_terms, 'blk', scatter_dimension=1, tiled=True)  112 us
    all_gather x1, waiting for transfers between devices, joined(): gathered = jax.tree.map(lambda a: lax.all_gather(a, axis), part)  112 us
    all_gather x2, blocking collectives, joined(): gathered = jax.tree.map(lambda a: lax.all_gather(a, axis), part)  73.6 us
    psum x1, blocking collectives, body(): lax.psum((cross_squares, cross_partial), 'blk')  56.7 us
    add x31, other arithmetic, combine(): earlier[2] * first_weight[..., None] + later[2] * second_weight[..., None]  44 us
    dynamic_slice x35, local copies, waits for them, and re-layouts, take(): lax.dynamic_index_in_dim(a, source, 0, False)  43.3 us
  transfers between devices with their start and end apart: 4, of which 4 were waited for; matrix products, arithmetic and copies ran while one was open for 2% of the time, Pallas kernels for 0%

commit v1 on v0

v1 whole, which is shorter than its diff:
```python
import functools

import jax
import jax.numpy as jnp
from jax import lax
from jax.experimental import pallas as pl
from jax.experimental.pallas import tpu as pltpu
from jax.sharding import PartitionSpec as P

MESH = pl.DeviceIdType.MESH
F32 = jnp.float32
BF16 = jnp.bfloat16
NEG = -1e30
EPS = 1e-06
LANES = 128
VMEM_BYTES = 64000000


def aligned(block, size=LANES):
    return pl.ds(pl.multiple_of(block * size, size), size)


def split3(x):
    high = x.astype(BF16).astype(F32)
    rest = x - high
    middle = rest.astype(BF16).astype(F32)
    return high, middle, rest - middle


def place(index, pieces):
    out = jnp.zeros(index.shape, F32)
    for at, piece in enumerate(pieces):
        out = jnp.where(index == at, piece, out)
    return out


NT = (((1,), (1,)), ((), ()))


def kernel(
    nb, nc, d_model,
    hid_ref, sgain_ref, cgain_ref, parents_ref, plen_ref,
    wself_hbm, wso_hbm, wcq_hbm, wco_hbm, cache_hbm, mem_hbm,
    out_ref,
    wself, wso, wcq, wco, wcop, cache, mem, vt_mem, kt, vt, lhs_q, lhs_p,
    s_a, g_a, s_c, g_c, s_d, r_d, s_e, r_e, s_f, r_f, s_q, g_q, s_g, r_g, s_h, g_h,
    load_sem,
    a_send, a_recv, c_send, c_recv, d_send, d_recv, e_send, e_recv,
    f_send, f_recv, q_send, q_recv, g_send, g_recv, h_send, h_recv,
):
    rows = hid_ref.shape[0]
    hyps = nb * rows
    half = nc // 2
    groups = half
    score_scale = 64 ** (-0.5)
    b = lax.axis_index("beam")
    c = lax.axis_index("blk")
    core = lax.rem(c, 2)
    partner = c + 1 - 2 * core

    loads = [
        pltpu.make_async_copy(cache_hbm, cache, load_sem.at[0]),
        pltpu.make_async_copy(wself_hbm.at[0], wself.at[:, pl.ds(0, LANES)], load_sem.at[1]),
        pltpu.make_async_copy(wself_hbm.at[1], wself.at[:, pl.ds(LANES, LANES)], load_sem.at[2]),
        pltpu.make_async_copy(wself_hbm.at[2], wself.at[:, pl.ds(2 * LANES, LANES)], load_sem.at[3]),
        pltpu.make_async_copy(mem_hbm, mem, load_sem.at[4]),
        pltpu.make_async_copy(wso_hbm, wso, load_sem.at[5]),
        pltpu.make_async_copy(wcq_hbm, wcq, load_sem.at[6]),
        pltpu.make_async_copy(wco_hbm, wco, load_sem.at[7]),
    ]
    for load in loads:
        load.start()

    barrier = pltpu.get_barrier_semaphore()

    def greet_blk(k, carry):
        pl.semaphore_signal(barrier, inc=1, device_id=(b, lax.rem(c + k, nc)), device_id_type=MESH)
        return carry

    def greet_beam(k, carry):
        pl.semaphore_signal(barrier, inc=1, device_id=(lax.rem(b + k, nb), c), device_id_type=MESH)
        return carry

    lax.fori_loop(1, nc, greet_blk, 0)
    lax.fori_loop(1, nb, greet_beam, 0)

    def remote(src, dst, send, recv, where):
        return pltpu.make_async_remote_copy(
            src_ref=src, dst_ref=dst, send_sem=send, recv_sem=recv, device_id=where, device_id_type=MESH
        )

    def gather_start(src, dst, send, recv):
        mine = dst.at[:, aligned(c)]
        remote(src, mine, send.at[0], recv.at[c], (b, partner)).start()

        def step(k, carry):
            remote(src, mine, send.at[k], recv.at[c], (b, lax.rem(c + 2 * k, nc))).start()
            return carry

        lax.fori_loop(1, half, step, 0)

    def gather_wait(src, dst, send, recv):
        def passed(k, carry):
            source = lax.rem(c + 2 * k, nc)
            block = dst.at[:, aligned(source)]
            remote(src, block, send.at[k], recv.at[source], (b, partner)).wait_recv()
            remote(block, block, send.at[half + k], recv.at[source], (b, partner)).start()
            return carry

        lax.fori_loop(1, half, passed, 0)

        def other(k, carry):
            source = lax.rem(partner + 2 * k, nc)
            block = dst.at[:, aligned(source)]
            remote(src, block, send.at[k], recv.at[source], (b, partner)).wait_recv()
            return carry

        lax.fori_loop(0, half, other, 0)

    def gather_drain(src, dst, send, recv):
        def step(k, carry):
            remote(src, dst.at[:, aligned(c)], send.at[k], recv.at[c], (b, partner)).wait_send()
            return carry

        lax.fori_loop(0, half, step, 0)

        def forwarded(k, carry):
            remote(src, dst.at[:, aligned(c)], send.at[half + k], recv.at[c], (b, partner)).wait_send()
            return carry

        lax.fori_loop(1, half, forwarded, 0)

    def scatter_start(src, dst, send, recv):
        def step(k, carry):
            target = lax.rem(c + k, nc)
            remote(src.at[:, aligned(target)], dst.at[c], send.at[k], recv.at[c], (b, target)).start()
            return carry

        lax.fori_loop(1, nc, step, 0)

    def scatter_sum(src, dst, send, recv):
        def step(k, total):
            source = lax.rem(c + k, nc)
            remote(src.at[:, aligned(c)], dst.at[source], send.at[k], recv.at[source], (b, source)).wait_recv()
            return total + dst[source].astype(F32)

        return lax.fori_loop(1, nc, step, src[:, aligned(c)].astype(F32))

    def scatter_drain(src, dst, send, recv):
        def step(k, carry):
            remote(src.at[:, aligned(c)], dst.at[c], send.at[k], recv.at[c], (b, partner)).wait_send()
            return carry

        lax.fori_loop(1, nc, step, 0)

    first = hid_ref[...]
    s_a[pl.ds(0, rows), :] = first
    gain_rows = jnp.broadcast_to(sgain_ref[...], (16, LANES))
    s_a[pl.ds(rows, 16), :] = gain_rows
    g_a[pl.ds(0, rows), aligned(c)] = first
    g_a[pl.ds(rows, 16), aligned(c)] = gain_rows
    pl.semaphore_wait(barrier, nc + nb - 2)
    gather_start(s_a, g_a, a_send, a_recv)

    loads[0].wait()
    width = 2 * cache.shape[0] // (2 * rows)

    def arrange(r, carry):
        x = cache[aligned(r, width), :].astype(F32)
        rolled = pltpu.roll(x, 64, 1)
        even = lax.rem(lax.broadcasted_iota(jnp.int32, x.shape, 0), 2) == 0
        low = lax.broadcasted_iota(jnp.int32, x.shape, 1) < 64
        keys = jnp.where(even, jnp.where(low, x, 0.0), jnp.where(low, 0.0, rolled))
        values = jnp.where(even, jnp.where(low, rolled, 0.0), jnp.where(low, 0.0, x))
        kt[:, aligned(r)] = keys.astype(BF16)
        vt[aligned(r, width), :] = values.astype(BF16)
        return carry

    lax.fori_loop(0, rows, arrange, 0)
    local_wide = jnp.broadcast_to(parents_ref[...], (LANES, hyps)).T - b * rows
    plen_wide = jnp.broadcast_to(plen_ref[...], (LANES, hyps)).T
    for load in loads[1:4]:
        load.wait()
    gather_wait(s_a, g_a, a_send, a_recv)

    wide = g_a[pl.ds(0, rows), :].astype(F32)
    gain = g_a[pl.ds(rows, 16), :].astype(F32)[0:1, :]
    self_mean = jnp.sum(wide * wide, axis=1, keepdims=True) * (1.0 / d_model)
    scaled = (wide * gain).astype(BF16)
    projected = jnp.dot(scaled, wself[...], preferred_element_type=F32) * lax.rsqrt(self_mean + EPS)
    projected = projected.astype(BF16)
    queries = projected[:, :LANES]

    s_c[...] = queries
    g_c[aligned(b, rows), :] = queries
    my_queries = g_c.at[aligned(b, rows), :]

    def send_c(k, carry):
        remote(s_c, my_queries, c_send.at[k], c_recv.at[b], (lax.rem(b + k, nb), c)).start()
        return carry

    lax.fori_loop(1, nb, send_c, 0)

    own_values = projected[:, 2 * LANES :].astype(F32)
    products = queries.astype(F32) * projected[:, LANES : 2 * LANES].astype(F32)
    low = lax.broadcasted_iota(jnp.int32, products.shape, 1) < 64
    own_0 = jnp.sum(jnp.where(low, products, 0.0), axis=1, keepdims=True) * score_scale
    own_1 = jnp.sum(jnp.where(low, 0.0, products), axis=1, keepdims=True) * score_scale

    loads[4].wait()
    head_width = mem.shape[1] // 2

    def turn(g, carry):
        block = mem[:, pl.ds(pl.multiple_of(head_width + g * 256, 256), 256)]
        vt_mem[aligned(g, 256), :] = block.T
        return carry

    lax.fori_loop(0, groups, turn, 0)

    def wait_c(k, carry):
        source = lax.rem(b + k, nb)
        remote(s_c, g_c.at[aligned(source, rows), :], c_send.at[k], c_recv.at[source], (source, c)).wait_recv()
        return carry

    lax.fori_loop(1, nb, wait_c, 0)

    all_queries = g_c[...].astype(F32)

    def spread_q(r, carry):
        lhs_q[:, aligned(r)] = jnp.where(local_wide == r, all_queries, 0.0).astype(BF16)
        return carry

    lax.fori_loop(0, rows, spread_q, 0)
    scores = lax.dot_general(lhs_q[...], kt[...], NT, preferred_element_type=F32) * score_scale
    lane = lax.broadcasted_iota(jnp.int32, scores.shape, 1)
    even = lax.rem(lane, 2) == 0
    tiles = width // LANES
    visible = lax.div(lane, 2) < jnp.concatenate([plen_wide] * tiles, axis=1)
    masked = jnp.where(visible, scores, NEG)
    max_0 = jnp.max(jnp.where(even, masked, NEG), axis=1, keepdims=True)
    max_1 = jnp.max(jnp.where(even, NEG, masked), axis=1, keepdims=True)
    weights = jnp.where(visible, jnp.exp(masked - jnp.where(even, max_0, max_1)), 0.0).astype(BF16).astype(F32)
    total_0 = jnp.sum(jnp.where(even, weights, 0.0), axis=1, keepdims=True)
    total_1 = jnp.sum(jnp.where(even, 0.0, weights), axis=1, keepdims=True)
    local_width = jnp.concatenate([local_wide] * tiles, axis=1)

    def spread_p(r, carry):
        lhs_p[:, aligned(r, width)] = jnp.where(local_width == r, weights, 0.0).astype(BF16)
        return carry

    lax.fori_loop(0, rows, spread_p, 0)
    summed = jnp.dot(lhs_p[...], vt[...], preferred_element_type=F32)
    lane = lax.broadcasted_iota(jnp.int32, summed.shape, 1)
    here = (local_wide >= 0) & (local_wide < rows)
    part = summed / jnp.where(lane < 64, total_0, total_1)
    pieces = split3(max_0 + jnp.log(total_0)) + split3(max_1 + jnp.log(total_1))
    s_d[:, pl.ds(0, LANES)] = part.astype(BF16)
    s_d[:, pl.ds(LANES, LANES)] = jnp.where(here, place(lane, pieces), 0.0).astype(BF16)

    def send_d(k, carry):
        target = lax.rem(b + k, nb)
        remote(s_d.at[aligned(target, rows), :], r_d.at[b], d_send.at[k], d_recv.at[b], (target, c)).start()
        return carry

    lax.fori_loop(1, nb, send_d, 0)

    loads[7].wait()
    quarter = 2 * rows

    def permute(g, carry):
        for which in range(2):
            for head in range(4):
                wcop[pl.ds(pl.multiple_of(g * 256 + which * 128 + head * 32, 32), 32), :] = wco[
                    pl.ds(pl.multiple_of(g * 256 + head * 64 + which * 32, 32), 32), :
                ]
        return carry

    lax.fori_loop(0, groups, permute, 0)
    loads[5].wait()
    loads[6].wait()

    def wait_d(k, total):
        source = lax.rem(b + k, nb)
        remote(s_d.at[aligned(b, rows), :], r_d.at[source], d_send.at[k], d_recv.at[source], (source, c)).wait_recv()
        return total + r_d[source].astype(F32)

    back = lax.fori_loop(1, nb, wait_d, s_d[aligned(b, rows), :].astype(F32))
    stats = back[:, LANES:]
    log_0 = stats[:, 0:1] + stats[:, 1:2] + stats[:, 2:3]
    log_1 = stats[:, 3:4] + stats[:, 4:5] + stats[:, 5:6]
    cache_log = jnp.where(low, log_0, log_1)
    own_log = jnp.where(low, own_0, own_1)
    top = jnp.maximum(cache_log, own_log)
    cache_weight = jnp.exp(cache_log - top)
    own_weight = jnp.exp(own_log - top)
    attended = (cache_weight * back[:, :LANES] + own_weight * own_values) / (cache_weight + own_weight)

    s_e[...] = jnp.dot(attended.astype(BF16), wso[...], preferred_element_type=F32).astype(BF16)
    scatter_start(s_e, r_e, e_send, e_recv)
    mixed = scatter_sum(s_e, r_e, e_send, e_recv)
    middle = (first.astype(F32) + mixed).astype(BF16).astype(F32)

    cross_scaled = (middle * cgain_ref[...].astype(F32)).astype(BF16)
    s_f[...] = jnp.dot(cross_scaled, wcq[...], preferred_element_type=F32).astype(BF16)
    scatter_start(s_f, r_f, f_send, f_recv)
    squares = jnp.broadcast_to(jnp.sum(middle * middle, axis=1, keepdims=True), (rows, LANES))
    squares = jnp.concatenate([squares] * (LANES // rows), axis=0).T[0:1, :]
    row16 = lax.broadcasted_iota(jnp.int32, (16, LANES), 0)
    square_rows = place(row16, split3(squares)).astype(BF16)
    s_q[pl.ds(rows, 16), :] = square_rows
    g_q[pl.ds(rows, 16), aligned(c)] = square_rows
    raw = scatter_sum(s_f, r_f, f_send, f_recv).astype(BF16)
    s_q[pl.ds(0, rows), :] = raw
    g_q[pl.ds(0, rows), aligned(c)] = raw
    gather_start(s_q, g_q, q_send, q_recv)
    gather_wait(s_q, g_q, q_send, q_recv)

    def add_squares(k, total):
        return total + g_q[pl.ds(rows, 16), aligned(k)].astype(F32)

    sums = lax.fori_loop(0, nc, add_squares, jnp.zeros((16, LANES), F32))
    mean = (sums[0:1, :] + sums[1:2, :] + sums[2:3, :]) * (1.0 / d_model)
    factor = lax.rsqrt(mean + EPS) * score_scale

    own_block = (
        lax.div(lax.broadcasted_iota(jnp.int32, (LANES, 256), 0), rows)
        == lax.div(lax.broadcasted_iota(jnp.int32, (LANES, 256), 1), 64)
    )
    lane_head = lax.div(lax.broadcasted_iota(jnp.int32, (64, LANES), 1), rows)

    def remember(i, carry):
        g = lax.rem(lax.div(c, 2) + 1 + i, groups)
        query = g_q[pl.ds(0, rows), aligned(g, 256)].astype(F32)
        query = jnp.where(own_block, jnp.concatenate([query] * 4, axis=0), 0.0).astype(BF16)
        score = lax.dot_general(mem[:, aligned(g, 256)], query, NT, preferred_element_type=F32) * factor
        most = jnp.max(score, axis=0, keepdims=True)
        weight = jnp.exp(score - most).astype(BF16)
        total = jnp.sum(weight.astype(F32), axis=0, keepdims=True)
        spread = jnp.dot(vt_mem[aligned(g, 256), :], weight, preferred_element_type=F32)
        taken = jnp.where(lane_head == 0, spread[0:64], 0.0)
        for head in range(1, 4):
            taken = jnp.where(lane_head == head, spread[head * 64 : head * 64 + 64], taken)
        stat = place(row16, split3(most) + split3(total)).astype(BF16)
        for which in range(2):
            target = 2 * g + which
            s_g[target, pl.ds(0, 32), :] = taken[which * 32 : which * 32 + 32].astype(BF16)
            s_g[target, pl.ds(32, 16), :] = stat

            @pl.when(target != c)
            def _():
                remote(
                    s_g.at[target], r_g.at[c], g_send.at[target], g_recv.at[c], (b, target)
                ).start()

        return carry

    lax.fori_loop(0, groups, remember, 0)
    r_g[c] = s_g[c]

    def wait_g(k, top):
        source = lax.rem(c + k, nc)
        remote(s_g.at[c], r_g.at[source], g_send.at[c], g_recv.at[source], (b, source)).wait_recv()
        stat = r_g[source, pl.ds(32, 16), :].astype(F32)
        return jnp.maximum(top, stat[0:1] + stat[1:2] + stat[2:3])

    stat = s_g[c, pl.ds(32, 16), :].astype(F32)
    top = lax.fori_loop(1, nc, wait_g, stat[0:1] + stat[1:2] + stat[2:3])
    over = jnp.zeros((32, LANES), F32)
    under = jnp.zeros((1, LANES), F32)
    for source in range(nc):
        stat = r_g[source, pl.ds(32, 16), :].astype(F32)
        share = jnp.exp(stat[0:1] + stat[1:2] + stat[2:3] - top)
        under = under + share * (stat[3:4] + stat[4:5] + stat[5:6])
        over = over + share * r_g[source, pl.ds(0, 32), :].astype(F32)
    turned = (over / under).T
    crossed = jnp.concatenate([turned[rows * head : rows * head + rows] for head in range(4)], axis=1).astype(BF16)

    s_h[...] = crossed
    g_h[:, aligned(c)] = crossed
    gather_start(s_h, g_h, h_send, h_recv)
    gather_wait(s_h, g_h, h_send, h_recv)
    out_ref[...] = (middle + jnp.dot(g_h[...], wcop[...], preferred_element_type=F32)).astype(BF16)

    gather_drain(s_a, g_a, a_send, a_recv)
    gather_drain(s_q, g_q, q_send, q_recv)
    gather_drain(s_h, g_h, h_send, h_recv)
    scatter_drain(s_e, r_e, e_send, e_recv)
    scatter_drain(s_f, r_f, f_send, f_recv)

    def drain_beam(k, carry):
        remote(s_c, my_queries, c_send.at[k], c_recv.at[b], (b, partner)).wait_send()
        remote(s_d.at[aligned(b, rows), :], r_d.at[b], d_send.at[k], d_recv.at[b], (b, partner)).wait_send()
        return carry

    lax.fori_loop(1, nb, drain_beam, 0)

    def drain_g(k, carry):
        target = lax.rem(c + k, nc)
        remote(s_g.at[target], r_g.at[c], g_send.at[target], g_recv.at[c], (b, target)).wait_send()
        return carry

    lax.fori_loop(1, nc, drain_g, 0)


def body(
    nb, nc, hidden_in, self_gain, w_self, w_self_out, cross_gain, w_cross_q, w_cross_out, cache_kv, memory_kv, parents, prefix_len
):
    rows = hidden_in.shape[0]
    d_model = w_self.shape[0]
    hyps = nb * rows
    cache_rows = cache_kv.shape[0] * cache_kv.shape[1] * cache_kv.shape[2]
    mem_count, mem_width = memory_kv.shape
    width = cache_rows // rows
    vmem = pl.BlockSpec(memory_space=pltpu.VMEM)
    hbm = pl.BlockSpec(memory_space=pl.ANY)
    wide = nc * LANES

    def v(*shape):
        return pltpu.VMEM(shape, BF16)

    def sems(count):
        return pltpu.SemaphoreType.DMA((count,))

    return pl.pallas_call(
        functools.partial(kernel, nb, nc, d_model),
        out_shape=jax.ShapeDtypeStruct((rows, LANES), BF16),
        in_specs=[vmem] * 5 + [hbm] * 6,
        out_specs=vmem,
        scratch_shapes=[
            v(d_model, 3 * LANES), v(LANES, wide), v(LANES, mem_width // 2), v(mem_width // 2, LANES), v(mem_width // 2, LANES),
            v(cache_rows, LANES), v(mem_count, mem_width), v(mem_width // 2, mem_count),
            v(width, rows * LANES), v(cache_rows, LANES), v(hyps, rows * LANES), v(hyps, rows * width),
            v(rows + 16, LANES), v(rows + 16, wide),
            v(rows, LANES), v(hyps, LANES),
            v(hyps, 2 * LANES), v(nb, rows, 2 * LANES),
            v(rows, wide), v(nc, rows, LANES),
            v(rows, wide), v(nc, rows, LANES),
            v(rows + 16, LANES), v(rows + 16, wide),
            v(nc, 48, LANES), v(nc, 48, LANES),
            v(rows, LANES), v(rows, wide),
            sems(8),
            sems(nc), sems(nc), sems(nb), sems(nb), sems(nb), sems(nb), sems(nc), sems(nc),
            sems(nc), sems(nc), sems(nc), sems(nc), sems(nc), sems(nc), sems(nc), sems(nc),
        ],
        compiler_params=pltpu.CompilerParams(
            collective_id=0, has_side_effects=True, vmem_limit_bytes=VMEM_BYTES
        ),
    )(
        hidden_in,
        self_gain.reshape(1, LANES),
        cross_gain.reshape(1, LANES),
        parents.reshape(1, hyps),
        prefix_len.reshape(1, hyps),
        jnp.transpose(w_self, (1, 0, 2)),
        w_self_out,
        w_cross_q,
        w_cross_out,
        cache_kv.reshape(cache_rows, LANES),
        memory_kv,
    )


def solution(mesh):
    return jax.shard_map(
        functools.partial(body, mesh.shape["beam"], mesh.shape["blk"]),
        mesh=mesh,
        in_specs=(
            P("beam", "blk"),
            P("blk"),
            P(None, None, "blk"),
            P("blk", None),
            P("blk"),
            P("blk", None),
            P(None, "blk"),
            P("beam", None, "blk", None),
            P("blk", None),
            P(),
            P(),
        ),
        out_specs=P("beam", "blk"),
        check_vma=False,
    )
```

time: 876 us -> 91.1 us (0.10)
  waiting for transfers between devices: 497 us -> 0 us
  blocking collectives: 200 us -> 0 us
  Pallas kernels: 0 us -> 89.7 us
  other arithmetic: 71.9 us -> 0 us
  local copies, waits for them, and re-layouts: 72 us -> 1.3 us
  matrix products: 13.3 us -> 0 us
  between operations: 13.3 us -> 0.01 us
    all_gather x2 -> x0, waiting for transfers between devices: 227 us -> none  [the longest x1 115 us: body(): shard_rows = lax.all_gather(cache_kv, 'beam', axis=0, tiled=True)]
    psum x1 -> x0, waiting for transfers between devices: 159 us -> none  [body(): lax.psum((cross_squares, cross_partial), 'blk')]
    all_gather x4 -> x0, blocking collectives: 144 us -> none  [the longest x2 73.6 us: joined(): gathered = jax.tree.map(lambda a: lax.all_gather(a, axis), part)]
    reduce_scatter x1 -> x0, waiting for transfers between devices: 112 us -> none  [body(): mixed = lax.psum_scatter(head_terms, 'blk', scatter_dimension=1, tiled=True)]
    pallas_call x0 -> x1, Pallas kernels: none -> 89.7 us  [body(): pl.pallas_call(functools.partial(kernel, nb, nc, d_model), out_shape=jax....]
    add x63 -> x0, other arithmetic: 67.5 us -> none  [the longest x31 44 us: combine(): earlier[2] * first_weight[..., None] + later[2] * second_weight[..., None]]
    psum x1 -> x0, blocking collectives: 56.7 us -> none  [body(): lax.psum((cross_squares, cross_partial), 'blk')]
    dynamic_slice x36 -> x0, local copies, waits for them, and re-layouts: 43.4 us -> none  [the longest x35 43.3 us: take(): lax.dynamic_index_in_dim(a, source, 0, False)]
  transfers between devices with their start and end apart: 4 -> 0, of which waited for: 4 -> 0; matrix products, arithmetic and copies ran while one was open for 2% -> 0% of each run, Pallas kernels for 0% -> 0%
where the time goes in v1:
time: 91.1 us; the launch traced here: 91 us
  Pallas kernels  89.7 us (98%)
  local copies, waits for them, and re-layouts  1.3 us (1%)
    pallas_call x1, Pallas kernels, body(): pl.pallas_call(functools.partial(kernel, nb, nc, d_model), out_shape=jax....  89.7 us

profile of v1, /device:TPU:1, one launch (start us, length us, event | category | flops | bytes accessed | tf_op | source)
XLA Modules:
  0.0 91.0 jit_solution(15973486894272306547)
XLA Ops:
  0.0 89.7 %shard_map.109 = bf16[32,128]{1,0:T(8,128)(2,1)} custom-call(bf16[32,128]{1,0:T(8,128)(2,1)} %hid_ref.1, bf16[1,128]{1,0:T(2,128)(2,1)} %bitcast.10, bf16[1,128]{1,0:T(2,128)(2,1)} %bitcast.11, s32[1,256]{1,0:T(1,128)} %bitcast.8, s32[1,256]{1,0:T(1,128)} %bitcast.9, bf16[3,4096,128]{2,1,0:T(8,128)(2,1)} %bitcast.6, bf16[128,4096]{1,0:T(8,128)(2,1)} %wso_hbm.1, ...), custom_call_target="tpu_custom_call" | custom-call | tf_op jit(solution)/shard_map/pallas_call | solution.py:424
  89.7 1.3 %copy.13 = bf16[32,128]{1,0:T(8,128)(2,1)} copy(bf16[32,128]{1,0:T(8,128)(2,1)} %shard_map.109) | data formatting | bytes 16384

commit v2 on v1

v2 whole, which is shorter than its diff:
```python
import functools

import jax
import jax.numpy as jnp
from jax import lax
from jax.experimental import pallas as pl
from jax.experimental.pallas import tpu as pltpu
from jax.sharding import PartitionSpec as P

MESH = pl.DeviceIdType.MESH
F32 = jnp.float32
BF16 = jnp.bfloat16
NEG = -1e30
EPS = 1e-06
LANES = 128
VMEM_BYTES = 64000000


def aligned(block, size=LANES):
    return pl.ds(pl.multiple_of(block * size, size), size)


def split3(x):
    high = x.astype(BF16).astype(F32)
    rest = x - high
    middle = rest.astype(BF16).astype(F32)
    return high, middle, rest - middle


def place(index, pieces):
    out = jnp.zeros(index.shape, F32)
    for at, piece in enumerate(pieces):
        out = jnp.where(index == at, piece, out)
    return out


NT = (((1,), (1,)), ((), ()))


def kernel(
    nb, nc, d_model,
    hid_ref, sgain_ref, cgain_ref, parents_ref, plen_ref,
    wself_hbm, wso_hbm, wcq_hbm, wco_hbm, cache_hbm, mem_hbm,
    out_ref,
    wself, wso, wcq, wco, cache, keys, values, vt_mem, kt, vt, lhs_q, acc,
    s_a, g_a, s_x, g_x, s_c, g_c, s_d, r_d, s_t, g_t, s_e, r_e, s_m, g_m, s_f, r_f, s_q, g_q, s_g, r_g, s_h, g_h,
    load_sem, swap_send, swap_recv,
    a_send, a_recv, c_send, c_recv, d_send, d_recv, e_send, e_recv,
    f_send, f_recv, q_send, q_recv, g_send, g_recv, h_send, h_recv,
):
    rows = hid_ref.shape[0]
    hyps = nb * rows
    half = nc // 2
    groups = half // 2
    score_scale = 64 ** (-0.5)
    head_width = mem_hbm.shape[1] // 2
    mem_rows = mem_hbm.shape[0]
    b = lax.axis_index("beam")
    c = lax.axis_index("blk")
    chip = lax.div(c, 2)
    core = lax.rem(c, 2)
    partner = c + 1 - 2 * core
    other_core = 1 - core
    steps = sorted(range(1, half), key=lambda k: -min(k % 8, 8 - k % 8))

    loads = [
        pltpu.make_async_copy(cache_hbm, cache, load_sem.at[0]),
        pltpu.make_async_copy(wself_hbm.at[0], wself.at[:, pl.ds(0, LANES)], load_sem.at[1]),
        pltpu.make_async_copy(wself_hbm.at[1], wself.at[:, pl.ds(LANES, LANES)], load_sem.at[2]),
        pltpu.make_async_copy(wself_hbm.at[2], wself.at[:, pl.ds(2 * LANES, LANES)], load_sem.at[3]),
        pltpu.make_async_copy(wco_hbm, wco, load_sem.at[4]),
    ]
    for load in loads:
        load.start()
    loaded = set()
    drains = []

    def ready(*which):
        for at in which:
            loads[at].wait()
            loaded.add(at)

    shared = [
        (wso_hbm, 0, wso, LANES), (wcq_hbm, 0, wcq, LANES),
        (mem_hbm, 0, keys, mem_rows), (mem_hbm, nc, values, mem_rows),
    ]

    def keep(g, carry):
        for at, (source, offset, target, height) in enumerate(shared):
            pltpu.make_async_copy(
                source.at[:, aligned(offset + 2 * g + core)],
                target.at[aligned(core, height), aligned(g)],
                load_sem.at[5 + at],
            ).start()
        return carry

    lax.fori_loop(0, half, keep, 0)

    barrier = pltpu.get_barrier_semaphore()

    def greet_blk(k, carry):
        pl.semaphore_signal(barrier, inc=1, device_id=(b, lax.rem(c + 2 * k, nc)), device_id_type=MESH)
        return carry

    def greet_beam(k, carry):
        pl.semaphore_signal(barrier, inc=1, device_id=(lax.rem(b + k, nb), c), device_id_type=MESH)
        return carry

    lax.fori_loop(1, half, greet_blk, 0)
    lax.fori_loop(1, nb, greet_beam, 0)
    pl.semaphore_signal(barrier, inc=1, device_id=(b, partner), device_id_type=MESH)

    def remote(src, dst, send, recv, where):
        return pltpu.make_async_remote_copy(
            src_ref=src, dst_ref=dst, send_sem=send, recv_sem=recv, device_id=where, device_id_type=MESH
        )

    def peer(k):
        return (b, lax.rem(c + 2 * k, nc))

    def chip_at(k):
        return lax.rem(chip + k, half)

    def swap_start():
        def step(at, g, carry):
            source, offset, target, height = shared[at]
            remote(
                source.at[:, aligned(offset + 2 * g + other_core)],
                target.at[aligned(core, height), aligned(g)],
                swap_send.at[at], swap_recv.at[at], (b, partner),
            ).start()
            return carry

        for at in range(len(shared)):
            lax.fori_loop(0, half, functools.partial(step, at), 0)

    def swapped(at, which):
        source, offset, target, height = shared[at]
        return remote(
            target.at[aligned(which, height), :], target.at[aligned(which, height), :],
            swap_send.at[at], swap_recv.at[at], (b, partner),
        )

    def swap_wait(at):
        source, offset, target, height = shared[at]
        mine = target.at[aligned(core, height), :]
        pltpu.make_async_copy(mine, mine, load_sem.at[5 + at]).wait()
        swapped(at, other_core).wait_recv()

    def swap_drain():
        for at in range(len(shared)):
            swapped(at, core).wait_send()

    def pair_start(src, dst, at):
        remote(src, dst.at[:, aligned(core)], swap_send.at[at], swap_recv.at[at], (b, partner)).start()
        drains.append(lambda: remote(src, dst.at[:, aligned(core)], swap_send.at[at], swap_recv.at[at], (b, partner)).wait_send())

    def pair_wait(src, dst, at):
        remote(src, dst.at[:, aligned(other_core)], swap_send.at[at], swap_recv.at[at], (b, partner)).wait_recv()

    def gather_start(src, dst, send, recv):
        mine = dst.at[:, aligned(c)]
        for k in steps:
            remote(src, mine, send.at[k], recv.at[c], peer(k)).start()
        remote(src, mine, send.at[0], recv.at[c], (b, partner)).start()
        drains.append(functools.partial(gather_drain, src, dst, send, recv))

    def gather_pass(src, dst, send, recv):
        for k in steps:
            source = lax.rem(c + 2 * (half - k), nc)
            block = dst.at[:, aligned(source)]
            remote(src, block, send.at[k], recv.at[source], (b, partner)).wait_recv()
            remote(block, block, send.at[half + k], recv.at[source], (b, partner)).start()

    def gather_wait(src, dst, send, recv):
        def other(k, carry):
            source = lax.rem(partner + 2 * k, nc)
            block = dst.at[:, aligned(source)]
            remote(src, block, send.at[0], recv.at[source], (b, partner)).wait_recv()
            return carry

        lax.fori_loop(0, half, other, 0)

    def gather_drain(src, dst, send, recv):
        def step(k, carry):
            remote(src, dst.at[:, aligned(c)], send.at[k], recv.at[c], (b, partner)).wait_send()
            return carry

        lax.fori_loop(0, half, step, 0)

        def forwarded(k, carry):
            remote(src, dst.at[:, aligned(c)], send.at[half + k], recv.at[c], (b, partner)).wait_send()
            return carry

        lax.fori_loop(1, half, forwarded, 0)

    def scatter_start(src, dst, send, recv):
        for k in steps:
            remote(src.at[:, aligned(chip_at(k))], dst.at[chip], send.at[k], recv.at[chip], peer(k)).start()
        drains.append(functools.partial(simple_drain, src.at[:, aligned(chip)], send))

    def simple_drain(block, send):
        def step(k, carry):
            remote(block, block, send.at[k], send.at[k], (b, partner)).wait_send()
            return carry

        lax.fori_loop(1, half, step, 0)

    def scatter_sum(src, dst, send, recv):
        total = src[:, aligned(chip)].astype(F32)
        for k in steps:
            source = chip_at(half - k)
            remote(src.at[:, aligned(chip)], dst.at[source], send.at[k], recv.at[source], (b, partner)).wait_recv()
            total = total + dst[source].astype(F32)
        return total

    first = hid_ref[...]
    gain_rows = jnp.broadcast_to(sgain_ref[...].astype(F32), (8, LANES)).astype(BF16)
    s_a[pl.ds(0, rows), :] = first
    s_a[pl.ds(rows, 8), :] = gain_rows
    g_a[pl.ds(0, rows), aligned(c)] = first
    g_a[pl.ds(rows, 8), aligned(c)] = gain_rows
    cgain_rows = jnp.broadcast_to(cgain_ref[...].astype(F32), (8, LANES))
    s_x[...] = cgain_rows
    g_x[:, aligned(core)] = cgain_rows
    pl.semaphore_wait(barrier, half + nb - 1)
    gather_start(s_a, g_a, a_send, a_recv)
    pair_start(s_x, g_x, 4)

    ready(0)
    width = cache.shape[0] // rows

    def arrange(r, carry):
        x = cache[aligned(r, width), :].astype(F32)
        rolled = pltpu.roll(x, 64, 1)
        even = lax.rem(lax.broadcasted_iota(jnp.int32, x.shape, 0), 2) == 0
        low = lax.broadcasted_iota(jnp.int32, x.shape, 1) < 64
        kt[:, aligned(r)] = jnp.where(even, jnp.where(low, x, 0.0), jnp.where(low, 0.0, rolled)).astype(BF16)
        vt[:, aligned(r)] = jnp.where(even, jnp.where(low, rolled, 0.0), jnp.where(low, 0.0, x)).astype(BF16)
        return carry

    lax.fori_loop(0, rows, arrange, 0)
    local_wide = jnp.broadcast_to(parents_ref[...], (LANES, hyps)).T - b * rows
    plen_wide = jnp.broadcast_to(plen_ref[...], (LANES, hyps)).T
    ready(1, 2, 3)
    gather_pass(s_a, g_a, a_send, a_recv)
    swap_start()
    drains.append(swap_drain)
    gather_wait(s_a, g_a, a_send, a_recv)

    wide = g_a[pl.ds(0, rows), :].astype(F32)
    gain = g_a[pl.ds(rows, 8), :].astype(F32)[0:1, :]
    self_scale = lax.rsqrt(jnp.sum(wide * wide, axis=1, keepdims=True) * (1.0 / d_model) + EPS)
    scaled = (wide * gain).astype(BF16)
    queries = (jnp.dot(scaled, wself[:, pl.ds(0, LANES)], preferred_element_type=F32) * self_scale).astype(BF16)

    s_c[...] = queries
    g_c[aligned(b, rows), :] = queries
    my_queries = g_c.at[aligned(b, rows), :]

    def send_c(k, carry):
        remote(s_c, my_queries, c_send.at[k], c_recv.at[b], (lax.rem(b + k, nb), c)).start()
        return carry

    lax.fori_loop(1, nb, send_c, 0)

    def drain_c():
        def step(k, carry):
            remote(s_c, my_queries, c_send.at[k], c_recv.at[b], (b, partner)).wait_send()
            return carry

        lax.fori_loop(1, nb, step, 0)

    drains.append(drain_c)
    projected = jnp.dot(scaled, wself[:, pl.ds(LANES, 2 * LANES)], preferred_element_type=F32) * self_scale
    projected = projected.astype(BF16).astype(F32)
    own_values = projected[:, LANES:]
    products = queries.astype(F32) * projected[:, :LANES]
    low = lax.broadcasted_iota(jnp.int32, products.shape, 1) < 64
    own_0 = jnp.sum(jnp.where(low, products, 0.0), axis=1, keepdims=True) * score_scale
    own_1 = jnp.sum(jnp.where(low, 0.0, products), axis=1, keepdims=True) * score_scale

    def wait_c(k, carry):
        source = lax.rem(b + k, nb)
        remote(s_c, g_c.at[aligned(source, rows), :], c_send.at[k], c_recv.at[source], (source, c)).wait_recv()
        return carry

    lax.fori_loop(1, nb, wait_c, 0)

    all_queries = g_c[...].astype(F32)

    def spread_q(r, carry):
        lhs_q[:, aligned(r)] = jnp.where(local_wide == r, all_queries, 0.0).astype(BF16)
        return carry

    lax.fori_loop(0, rows, spread_q, 0)
    scores = lax.dot_general(lhs_q[...], kt[...], NT, preferred_element_type=F32) * score_scale
    lane = lax.broadcasted_iota(jnp.int32, scores.shape, 1)
    even = lax.rem(lane, 2) == 0
    tiles = width // LANES
    visible = lax.div(lane, 2) < jnp.concatenate([plen_wide] * tiles, axis=1)
    masked = jnp.where(visible, scores, NEG)
    max_0 = jnp.max(jnp.where(even, masked, NEG), axis=1, keepdims=True)
    max_1 = jnp.max(jnp.where(even, NEG, masked), axis=1, keepdims=True)
    weights = jnp.where(visible, jnp.exp(masked - jnp.where(even, max_0, max_1)), 0.0).astype(BF16)
    lhs_q[:, pl.ds(0, width)] = weights
    weights = weights.astype(F32)
    total_0 = jnp.sum(jnp.where(even, weights, 0.0), axis=1, keepdims=True)
    total_1 = jnp.sum(jnp.where(even, 0.0, weights), axis=1, keepdims=True)
    acc[...] = jnp.zeros(acc.shape, F32)

    def select(r, carry):
        both = jnp.dot(lhs_q[:, pl.ds(0, width)], vt[:, aligned(r, 2 * LANES)], preferred_element_type=F32)
        picked = jnp.where(local_wide == 2 * r, both[:, :LANES], acc[...])
        acc[...] = jnp.where(local_wide == 2 * r + 1, both[:, LANES:], picked)
        return carry

    lax.fori_loop(0, rows // 2, select, 0)
    summed = acc[...]
    lane = lax.broadcasted_iota(jnp.int32, summed.shape, 1)
    here = (local_wide >= 0) & (local_wide < rows)
    part = summed / jnp.where(lane < 64, total_0, total_1)
    pieces = split3(max_0 + jnp.log(total_0)) + split3(max_1 + jnp.log(total_1))
    s_d[:, pl.ds(0, LANES)] = part.astype(BF16)
    s_d[:, pl.ds(LANES, LANES)] = jnp.where(here, place(lane, pieces), 0.0).astype(BF16)

    def send_d(k, carry):
        target = lax.rem(b + k, nb)
        remote(s_d.at[aligned(target, rows), :], r_d.at[b], d_send.at[k], d_recv.at[b], (target, c)).start()
        return carry

    lax.fori_loop(1, nb, send_d, 0)

    def drain_d():
        def step(k, carry):
            remote(s_d.at[aligned(b, rows), :], r_d.at[b], d_send.at[k], d_recv.at[b], (b, partner)).wait_send()
            return carry

        lax.fori_loop(1, nb, step, 0)

    drains.append(drain_d)
    swap_wait(0)
    swap_wait(1)
    ready(4)

    def wait_d(k, total):
        source = lax.rem(b + k, nb)
        remote(s_d.at[aligned(b, rows), :], r_d.at[source], d_send.at[k], d_recv.at[source], (source, c)).wait_recv()
        return total + r_d[source].astype(F32)

    back = lax.fori_loop(1, nb, wait_d, s_d[aligned(b, rows), :].astype(F32))
    stats = back[:, LANES:]
    log_0 = stats[:, 0:1] + stats[:, 1:2] + stats[:, 2:3]
    log_1 = stats[:, 3:4] + stats[:, 4:5] + stats[:, 5:6]
    cache_log = jnp.where(low, log_0, log_1)
    own_log = jnp.where(low, own_0, own_1)
    top = jnp.maximum(cache_log, own_log)
    cache_weight = jnp.exp(cache_log - top)
    own_weight = jnp.exp(own_log - top)
    attended = (cache_weight * back[:, :LANES] + own_weight * own_values) / (cache_weight + own_weight)
    attended = attended.astype(BF16)
    s_t[...] = attended
    g_t[:, aligned(core)] = attended
    pair_start(s_t, g_t, 5)
    pair_wait(s_t, g_t, 5)

    s_e[...] = jnp.dot(g_t[...], wso[...], preferred_element_type=F32).astype(BF16)
    scatter_start(s_e, r_e, e_send, e_recv)
    swap_wait(2)
    swap_wait(3)

    def turn(g, carry):
        vt_mem[aligned(g, 256), :] = values[:, aligned(g, 256)].T
        return carry

    lax.fori_loop(0, groups, turn, 0)
    mixed = scatter_sum(s_e, r_e, e_send, e_recv)
    middle_16 = (first.astype(F32) + mixed).astype(BF16)
    middle = middle_16.astype(F32)

    s_m[...] = middle_16
    g_m[:, aligned(core)] = middle_16
    pair_start(s_m, g_m, 6)
    pair_wait(s_x, g_x, 4)
    pair_wait(s_m, g_m, 6)
    both_middle = g_m[...].astype(F32)
    cross_scaled = (both_middle * g_x[0:1, :]).astype(BF16)
    s_f[...] = jnp.dot(cross_scaled, wcq[...], preferred_element_type=F32).astype(BF16)
    scatter_start(s_f, r_f, f_send, f_recv)
    squares = jnp.broadcast_to(jnp.sum(both_middle * both_middle, axis=1, keepdims=True), (rows, LANES))
    squares = jnp.concatenate([squares] * (LANES // rows), axis=0).T[0:1, :]
    row8 = lax.broadcasted_iota(jnp.int32, (8, LANES), 0)
    square_rows = place(row8, split3(squares)).astype(BF16)
    s_q[pl.ds(rows, 8), :] = square_rows
    g_q[pl.ds(rows, 8), aligned(chip)] = square_rows
    raw = scatter_sum(s_f, r_f, f_send, f_recv).astype(BF16)
    s_q[pl.ds(0, rows), :] = raw
    g_q[pl.ds(0, rows), aligned(chip)] = raw

    for k in steps:
        remote(s_q, g_q.at[:, aligned(chip)], q_send.at[k], q_recv.at[chip], peer(k)).start()
    drains.append(functools.partial(simple_drain, s_q, q_send))
    for k in steps:
        source = chip_at(half - k)
        remote(s_q, g_q.at[:, aligned(source)], q_send.at[k], q_recv.at[source], (b, partner)).wait_recv()
    sums = jnp.zeros((8, LANES), F32)
    for k in range(half):
        sums = sums + g_q[pl.ds(rows, 8), pl.ds(k * LANES, LANES)].astype(F32)
    mean = (sums[0:1, :] + sums[1:2, :] + sums[2:3, :]) * (1.0 / d_model)
    factor = lax.rsqrt(mean + EPS) * score_scale

    own_block = (
        lax.div(lax.broadcasted_iota(jnp.int32, (LANES, 256), 0), rows)
        == lax.div(lax.broadcasted_iota(jnp.int32, (LANES, 256), 1), 64)
    )
    lane_head = lax.div(lax.broadcasted_iota(jnp.int32, (64, LANES), 1), rows)
    left = lax.broadcasted_iota(jnp.int32, (32, LANES), 1) < 64

    def deliver(g):
        for which in range(2):
            target = 2 * g + which

            @pl.when(target != chip)
            def _():
                remote(
                    s_g.at[target], r_g.at[chip], g_send.at[target], g_recv.at[chip], (b, 2 * target + core)
                ).start()

    offsets = sorted(range(groups), key=lambda k: -min(k % 4, 4 - k % 4) if k else 1)
    previous = None
    for offset in offsets:
        g = lax.rem(lax.div(chip, 2) + offset, groups)
        query = g_q[pl.ds(0, rows), aligned(g, 256)].astype(F32)
        query = jnp.where(own_block, jnp.concatenate([query] * 4, axis=0), 0.0).astype(BF16)
        score = lax.dot_general(keys[:, aligned(g, 256)], query, NT, preferred_element_type=F32) * factor
        most = jnp.max(score, axis=0, keepdims=True)
        weight = jnp.exp(score - most).astype(BF16)
        total = jnp.sum(weight.astype(F32), axis=0, keepdims=True)
        spread = jnp.dot(vt_mem[aligned(g, 256), :], weight, preferred_element_type=F32)
        taken = jnp.where(lane_head == 0, spread[0:64], 0.0)
        for head in range(1, 4):
            taken = jnp.where(lane_head == head, spread[head * 64 : head * 64 + 64], taken)
        stat = place(row8, split3(most) + split3(total))
        turned = pltpu.roll(taken, 64, 1)
        turned_stat = pltpu.roll(stat, 64, 1)
        s_g[2 * g, pl.ds(0, 32), :] = jnp.where(left, taken[0:32], turned[32:64]).astype(BF16)
        s_g[2 * g, pl.ds(32, 8), :] = jnp.where(left[0:8], stat, turned_stat).astype(BF16)
        s_g[2 * g + 1, pl.ds(0, 32), :] = jnp.where(left, turned[0:32], taken[32:64]).astype(BF16)
        s_g[2 * g + 1, pl.ds(32, 8), :] = jnp.where(left[0:8], turned_stat, stat).astype(BF16)
        if previous is not None:
            deliver(previous)
        previous = g
    deliver(previous)
    r_g[chip] = s_g[chip]

    def drain_g():
        for k in steps:
            target = chip_at(k)
            remote(s_g.at[target], r_g.at[chip], g_send.at[target], g_recv.at[chip], peer(k)).wait_send()

    drains.append(drain_g)
    for k in steps:
        source = chip_at(half - k)
        remote(s_g.at[chip], r_g.at[source], g_send.at[chip], g_recv.at[source], peer(half - k)).wait_recv()
    stats = [r_g[source, pl.ds(32, 8), :].astype(F32) for source in range(half)]
    mosts = [stat[0:1] + stat[1:2] + stat[2:3] for stat in stats]
    top = functools.reduce(jnp.maximum, mosts)
    over = jnp.zeros((32, LANES), F32)
    under = jnp.zeros((1, LANES), F32)
    for source in range(half):
        share = jnp.exp(mosts[source] - top)
        stat = stats[source]
        under = under + share * (stat[3:4] + stat[4:5] + stat[5:6])
        over = over + share * r_g[source, pl.ds(0, 32), :].astype(F32)
    turned = (over / under).T
    crossed = jnp.concatenate([turned[rows * at : rows * at + rows] for at in (0, 2, 1, 3)], axis=1).astype(BF16)

    s_h[...] = crossed
    g_h[:, aligned(c)] = crossed
    gather_start(s_h, g_h, h_send, h_recv)
    gather_pass(s_h, g_h, h_send, h_recv)
    gather_wait(s_h, g_h, h_send, h_recv)
    out_ref[...] = (middle + jnp.dot(g_h[...], wco[...], preferred_element_type=F32)).astype(BF16)

    for drain in drains:
        drain()


def body(
    nb, nc, hidden_in, self_gain, w_self, w_self_out, cross_gain, w_cross_q, w_cross_out, cache_kv, memory_kv, parents, prefix_len
):
    rows = hidden_in.shape[0]
    d_model = w_self.shape[0]
    hyps = nb * rows
    cache_rows = cache_kv.shape[0] * cache_kv.shape[1] * cache_kv.shape[2]
    mem_count, mem_width = memory_kv.shape
    width = cache_rows // rows
    vmem = pl.BlockSpec(memory_space=pltpu.VMEM)
    hbm = pl.BlockSpec(memory_space=pl.ANY)
    wide = nc * LANES
    chips = nc // 2

    def v(*shape):
        return pltpu.VMEM(shape, BF16)

    def sems(count):
        return pltpu.SemaphoreType.DMA((count,))

    return pl.pallas_call(
        functools.partial(kernel, nb, nc, d_model),
        out_shape=jax.ShapeDtypeStruct((rows, LANES), BF16),
        in_specs=[vmem] * 5 + [hbm] * 6,
        out_specs=vmem,
        scratch_shapes=[
            v(d_model, 3 * LANES), v(2 * LANES, wide // 2), v(2 * LANES, wide // 2), v(mem_width // 2, LANES),
            v(cache_rows, LANES), v(2 * mem_count, wide // 2), v(2 * mem_count, wide // 2), v(wide // 2, 2 * mem_count),
            v(width, rows * LANES), v(width, rows * LANES), v(hyps, rows * LANES), pltpu.VMEM((hyps, LANES), F32),
            v(rows + 8, LANES), v(rows + 8, wide), pltpu.VMEM((8, LANES), F32), pltpu.VMEM((8, 2 * LANES), F32),
            v(rows, LANES), v(hyps, LANES),
            v(hyps, 2 * LANES), v(nb, rows, 2 * LANES),
            v(rows, LANES), v(rows, 2 * LANES),
            v(rows, wide // 2), v(chips, rows, LANES),
            v(rows, LANES), v(rows, 2 * LANES),
            v(rows, wide // 2), v(chips, rows, LANES),
            v(rows + 8, LANES), v(rows + 8, wide // 2),
            v(chips, 40, LANES), v(chips, 40, LANES),
            v(rows, LANES), v(rows, wide),
            sems(9), sems(7), sems(7),
            sems(nc), sems(nc), sems(nb), sems(nb), sems(nb), sems(nb), sems(chips), sems(chips),
            sems(chips), sems(chips), sems(chips), sems(chips), sems(chips), sems(chips), sems(nc), sems(nc),
        ],
        compiler_params=pltpu.CompilerParams(
            collective_id=0, has_side_effects=True, vmem_limit_bytes=VMEM_BYTES
        ),
    )(
        hidden_in,
        self_gain.reshape(1, LANES),
        cross_gain.reshape(1, LANES),
        parents.reshape(1, hyps),
        prefix_len.reshape(1, hyps),
        jnp.transpose(w_self, (1, 0, 2)),
        w_self_out,
        w_cross_q,
        w_cross_out,
        cache_kv.reshape(cache_rows, LANES),
        memory_kv,
    )


def solution(mesh):
    return jax.shard_map(
        functools.partial(body, mesh.shape["beam"], mesh.shape["blk"]),
        mesh=mesh,
        in_specs=(
            P("beam", "blk"),
            P("blk"),
            P(None, None, "blk"),
            P("blk", None),
            P("blk"),
            P("blk", None),
            P(None, "blk"),
            P("beam", None, "blk", None),
            P("blk", None),
            P(),
            P(),
        ),
        out_specs=P("beam", "blk"),
        check_vma=False,
    )
```

time: 91.1 us -> 74.3 us (0.82)
  Pallas kernels: 89.7 us -> 72.8 us
    pallas_call x1, Pallas kernels: 89.7 us -> 72.8 us  [body(): pl.pallas_call(functools.partial(kernel, nb, nc, d_model), out_shape=jax....]
where the time goes in v2:
time: 74.3 us; the launch traced here: 74.1 us
  Pallas kernels  72.8 us (98%)
  local copies, waits for them, and re-layouts  1.3 us (2%)
    pallas_call x1, Pallas kernels, body(): pl.pallas_call(functools.partial(kernel, nb, nc, d_model), out_shape=jax....  72.8 us

profile of v2, /device:TPU:1, one launch (start us, length us, event | category | flops | bytes accessed | tf_op | source)
XLA Modules:
  0.0 74.1 jit_solution(902888305282855434)
XLA Ops:
  0.0 72.8 %shard_map.109 = bf16[32,128]{1,0:T(8,128)(2,1)} custom-call(bf16[32,128]{1,0:T(8,128)(2,1)} %hid_ref.1, bf16[1,128]{1,0:T(2,128)(2,1)} %bitcast.10, bf16[1,128]{1,0:T(2,128)(2,1)} %bitcast.11, s32[1,256]{1,0:T(1,128)} %bitcast.8, s32[1,256]{1,0:T(1,128)} %bitcast.9, bf16[3,4096,128]{2,1,0:T(8,128)(2,1)} %bitcast.6, bf16[128,4096]{1,0:T(8,128)(2,1)} %wso_hbm.1, ...), custom_call_target="tpu_custom_call" | custom-call | tf_op jit(solution)/shard_map/pallas_call | solution.py:509
  72.8 1.3 %copy.13 = bf16[32,128]{1,0:T(8,128)(2,1)} copy(bf16[32,128]{1,0:T(8,128)(2,1)} %shard_map.109) | data formatting | bytes 16384

commit v3 on v2

--- a/solution.py
+++ b/solution.py
@@ -39,16 +39,17 @@
 
 def kernel(
     nb, nc, d_model,
-    hid_ref, sgain_ref, cgain_ref, parents_ref, plen_ref,
+    hid_hbm, sgain_hbm, cgain_hbm, parents_hbm, plen_hbm,
     wself_hbm, wso_hbm, wcq_hbm, wco_hbm, cache_hbm, mem_hbm,
-    out_ref,
+    out_hbm,
+    sgain, cgain, parents, plen, result,
     wself, wso, wcq, wco, cache, keys, values, vt_mem, kt, vt, lhs_q, acc,
-    s_a, g_a, s_x, g_x, s_c, g_c, s_d, r_d, s_t, g_t, s_e, r_e, s_m, g_m, s_f, r_f, s_q, g_q, s_g, r_g, s_h, g_h,
+    s_a, g_a, s_x, g_x, s_c, g_c, s_d, r_d, s_t, g_t, s_e, r_e, s_m, g_m, s_f, r_f, s_q, g_q, s_g, r_g, s_h, g_h, s_p, r_p, s_o, r_o,
     load_sem, swap_send, swap_recv,
     a_send, a_recv, c_send, c_recv, d_send, d_recv, e_send, e_recv,
     f_send, f_recv, q_send, q_recv, g_send, g_recv, h_send, h_recv,
 ):
-    rows = hid_ref.shape[0]
+    rows = hid_hbm.shape[0]
     hyps = nb * rows
     half = nc // 2
     groups = half // 2
@@ -63,52 +64,72 @@
     other_core = 1 - core
     steps = sorted(range(1, half), key=lambda k: -min(k % 8, 8 - k % 8))
 
+    barrier = pltpu.get_barrier_semaphore()
+
+    def greet_blk(k, carry):
+        pl.semaphore_signal(barrier, inc=1, device_id=(b, lax.rem(c + 2 * k, nc)), device_id_type=MESH)
+        return carry
+
+    def greet_beam(k, carry):
+        pl.semaphore_signal(barrier, inc=1, device_id=(lax.rem(b + k, nb), c), device_id_type=MESH)
+        return carry
+
+    lax.fori_loop(1, half, greet_blk, 0)
+    lax.fori_loop(1, nb, greet_beam, 0)
+    pl.semaphore_signal(barrier, inc=1, device_id=(b, partner), device_id_type=MESH)
+
     loads = [
-        pltpu.make_async_copy(cache_hbm, cache, load_sem.at[0]),
-        pltpu.make_async_copy(wself_hbm.at[0], wself.at[:, pl.ds(0, LANES)], load_sem.at[1]),
-        pltpu.make_async_copy(wself_hbm.at[1], wself.at[:, pl.ds(LANES, LANES)], load_sem.at[2]),
-        pltpu.make_async_copy(wself_hbm.at[2], wself.at[:, pl.ds(2 * LANES, LANES)], load_sem.at[3]),
-        pltpu.make_async_copy(wco_hbm, wco, load_sem.at[4]),
+        pltpu.make_async_copy(hid_hbm, s_a.at[pl.ds(0, rows), :], load_sem.at[0]),
+        pltpu.make_async_copy(sgain_hbm, sgain, load_sem.at[1]),
+        pltpu.make_async_copy(cgain_hbm, cgain, load_sem.at[2]),
+        pltpu.make_async_copy(parents_hbm, parents, load_sem.at[3]),
+        pltpu.make_async_copy(plen_hbm, plen, load_sem.at[4]),
+        pltpu.make_async_copy(cache_hbm, cache, load_sem.at[5]),
     ]
     for load in loads:
         load.start()
     loaded = set()
     drains = []
+    swap_done = set()
+    swap_begun = set()
+    pair_open = []
 
     def ready(*which):
         for at in which:
             loads[at].wait()
             loaded.add(at)
 
+    def columns(source, target, offset=0):
+        height = source.shape[0]
+        return (
+            lambda g, side: source.at[:, aligned(offset + 2 * g + side)],
+            lambda g, who: target.at[aligned(who, height), aligned(g)],
+            lambda who: target.at[aligned(who, height), :],
+        )
+
+    def kind(which):
+        return (
+            lambda g, side: wself_hbm.at[which, aligned(2 * g + side), :],
+            lambda g, who: wself.at[aligned(g), aligned(3 * who + which)],
+            lambda who: wself.at[:, aligned(3 * who + which)],
+        )
+
+    out_rows = (
+        lambda g, side: wco_hbm.at[aligned(2 * g + side), :],
+        lambda g, who: wco.at[aligned(g), aligned(who)],
+        lambda who: wco.at[:, aligned(who)],
+    )
     shared = [
-        (wso_hbm, 0, wso, LANES), (wcq_hbm, 0, wcq, LANES),
-        (mem_hbm, 0, keys, mem_rows), (mem_hbm, nc, values, mem_rows),
+        kind(0), kind(1), kind(2), columns(wso_hbm, wso), columns(wcq_hbm, wcq),
+        columns(mem_hbm, keys), columns(mem_hbm, values, nc), out_rows,
     ]
 
     def keep(g, carry):
-        for at, (source, offset, target, height) in enumerate(shared):
-            pltpu.make_async_copy(
-                source.at[:, aligned(offset + 2 * g + core)],
-                target.at[aligned(core, height), aligned(g)],
-                load_sem.at[5 + at],
-            ).start()
+        for at, (block, place_at, whole) in enumerate(shared):
+            pltpu.make_async_copy(block(g, core), place_at(g, core), load_sem.at[6 + at]).start()
         return carry
 
     lax.fori_loop(0, half, keep, 0)
-
-    barrier = pltpu.get_barrier_semaphore()
-
-    def greet_blk(k, carry):
-        pl.semaphore_signal(barrier, inc=1, device_id=(b, lax.rem(c + 2 * k, nc)), device_id_type=MESH)
-        return carry
-
-    def greet_beam(k, carry):
-        pl.semaphore_signal(barrier, inc=1, device_id=(lax.rem(b + k, nb), c), device_id_type=MESH)
-        return carry
-
-    lax.fori_loop(1, half, greet_blk, 0)
-    lax.fori_loop(1, nb, greet_beam, 0)
-    pl.semaphore_signal(barrier, inc=1, device_id=(b, partner), device_id_type=MESH)
 
     def remote(src, dst, send, recv, where):
         return pltpu.make_async_remote_copy(
@@ -121,78 +142,54 @@
     def chip_at(k):
         return lax.rem(chip + k, half)
 
-    def swap_start():
-        def step(at, g, carry):
-            source, offset, target, height = shared[at]
-            remote(
-                source.at[:, aligned(offset + 2 * g + other_core)],
-                target.at[aligned(core, height), aligned(g)],
-                swap_send.at[at], swap_recv.at[at], (b, partner),
-            ).start()
+    def swap_start(*which):
+        def step(g, carry):
+            for at in which:
+                block, place_at, whole = shared[at]
+                remote(
+                    block(g, other_core), place_at(g, core), swap_send.at[at], swap_recv.at[at], (b, partner)
+                ).start()
             return carry
 
-        for at in range(len(shared)):
-            lax.fori_loop(0, half, functools.partial(step, at), 0)
-
-    def swapped(at, which):
-        source, offset, target, height = shared[at]
-        return remote(
-            target.at[aligned(which, height), :], target.at[aligned(which, height), :],
-            swap_send.at[at], swap_recv.at[at], (b, partner),
-        )
-
-    def swap_wait(at):
-        source, offset, target, height = shared[at]
-        mine = target.at[aligned(core, height), :]
-        pltpu.make_async_copy(mine, mine, load_sem.at[5 + at]).wait()
-        swapped(at, other_core).wait_recv()
-
-    def swap_drain():
-        for at in range(len(shared)):
-            swapped(at, core).wait_send()
+        lax.fori_loop(0, half, step, 0)
+        swap_begun.update(which)
+
+        def drain():
+            for at in which:
+                mine = shared[at][2](core)
+                remote(mine, mine, swap_send.at[at], swap_recv.at[at], (b, partner)).wait_send()
+
+        drains.append(drain)
+
+    def swap_wait(*which):
+        for at in which:
+            swap_done.add(at)
+            mine, theirs = shared[at][2](core), shared[at][2](other_core)
+            pltpu.make_async_copy(mine, mine, load_sem.at[6 + at]).wait()
+            if at in swap_begun:
+                remote(theirs, theirs, swap_send.at[at], swap_recv.at[at], (b, partner)).wait_recv()
+
+    def pair(src, dst, at):
+        return remote(src, dst, swap_send.at[at], swap_recv.at[at], (b, partner))
 
     def pair_start(src, dst, at):
-        remote(src, dst.at[:, aligned(core)], swap_send.at[at], swap_recv.at[at], (b, partner)).start()
-        drains.append(lambda: remote(src, dst.at[:, aligned(core)], swap_send.at[at], swap_recv.at[at], (b, partner)).wait_send())
+        pair(src, dst, at).start()
+        pair_open.append((src, dst, at))
+        drains.append(lambda: pair(src, dst, at).wait_send())
 
     def pair_wait(src, dst, at):
-        remote(src, dst.at[:, aligned(other_core)], swap_send.at[at], swap_recv.at[at], (b, partner)).wait_recv()
+        pair_open[:] = [p for p in pair_open if p[2] != at]
+        pair(src, dst, at).wait_recv()
 
     def gather_start(src, dst, send, recv):
-        mine = dst.at[:, aligned(c)]
         for k in steps:
-            remote(src, mine, send.at[k], recv.at[c], peer(k)).start()
-        remote(src, mine, send.at[0], recv.at[c], (b, partner)).start()
-        drains.append(functools.partial(gather_drain, src, dst, send, recv))
-
-    def gather_pass(src, dst, send, recv):
+            remote(src, dst.at[:, aligned(chip)], send.at[k], recv.at[chip], peer(k)).start()
+        drains.append(functools.partial(simple_drain, src, send))
+
+    def gather_wait(src, dst, send, recv):
         for k in steps:
-            source = lax.rem(c + 2 * (half - k), nc)
-            block = dst.at[:, aligned(source)]
-            remote(src, block, send.at[k], recv.at[source], (b, partner)).wait_recv()
-            remote(block, block, send.at[half + k], recv.at[source], (b, partner)).start()
-
-    def gather_wait(src, dst, send, recv):
-        def other(k, carry):
-            source = lax.rem(partner + 2 * k, nc)
-            block = dst.at[:, aligned(source)]
-            remote(src, block, send.at[0], recv.at[source], (b, partner)).wait_recv()
-            return carry
-
-        lax.fori_loop(0, half, other, 0)
-
-    def gather_drain(src, dst, send, recv):
-        def step(k, carry):
-            remote(src, dst.at[:, aligned(c)], send.at[k], recv.at[c], (b, partner)).wait_send()
-            return carry
-
-        lax.fori_loop(0, half, step, 0)
-
-        def forwarded(k, carry):
-            remote(src, dst.at[:, aligned(c)], send.at[half + k], recv.at[c], (b, partner)).wait_send()
-            return carry
-
-        lax.fori_loop(1, half, forwarded, 0)
+            source = chip_at(half - k)
+            remote(src, dst.at[:, aligned(source)], send.at[k], recv.at[source], (b, partner)).wait_recv()
 
     def scatter_start(src, dst, send, recv):
         for k in steps:
@@ -214,20 +211,21 @@
             total = total + dst[source].astype(F32)
         return total
 
-    first = hid_ref[...]
-    gain_rows = jnp.broadcast_to(sgain_ref[...].astype(F32), (8, LANES)).astype(BF16)
-    s_a[pl.ds(0, rows), :] = first
+    ready(0, 1, 2)
+    first = s_a[pl.ds(0, rows), :]
+    gain_rows = jnp.broadcast_to(sgain[...].astype(F32), (8, LANES)).astype(BF16)
     s_a[pl.ds(rows, 8), :] = gain_rows
-    g_a[pl.ds(0, rows), aligned(c)] = first
-    g_a[pl.ds(rows, 8), aligned(c)] = gain_rows
-    cgain_rows = jnp.broadcast_to(cgain_ref[...].astype(F32), (8, LANES))
+    g_a[pl.ds(0, rows), aligned(chip)] = first
+    g_a[pl.ds(rows, 8), aligned(chip)] = gain_rows
+    cgain_rows = jnp.broadcast_to(cgain[...].astype(F32), (8, LANES))
     s_x[...] = cgain_rows
     g_x[:, aligned(core)] = cgain_rows
     pl.semaphore_wait(barrier, half + nb - 1)
     gather_start(s_a, g_a, a_send, a_recv)
-    pair_start(s_x, g_x, 4)
-
-    ready(0)
+    pair_start(s_x, g_x.at[:, aligned(core)], 8)
+    swap_start(0, 1, 2)
+
+    ready(5)
     width = cache.shape[0] // rows
 
     def arrange(r, carry):
@@ -240,19 +238,25 @@
         return carry
 
     lax.fori_loop(0, rows, arrange, 0)
-    local_wide = jnp.broadcast_to(parents_ref[...], (LANES, hyps)).T - b * rows
-    plen_wide = jnp.broadcast_to(plen_ref[...], (LANES, hyps)).T
-    ready(1, 2, 3)
-    gather_pass(s_a, g_a, a_send, a_recv)
-    swap_start()
-    drains.append(swap_drain)
+    ready(3, 4)
+    local_wide = jnp.broadcast_to(parents[...], (LANES, hyps)).T - b * rows
+    plen_wide = jnp.broadcast_to(plen[...], (LANES, hyps)).T
+    swap_wait(0, 1, 2)
     gather_wait(s_a, g_a, a_send, a_recv)
 
     wide = g_a[pl.ds(0, rows), :].astype(F32)
     gain = g_a[pl.ds(rows, 8), :].astype(F32)[0:1, :]
-    self_scale = lax.rsqrt(jnp.sum(wide * wide, axis=1, keepdims=True) * (1.0 / d_model) + EPS)
+    squares = jnp.broadcast_to(jnp.sum(wide * wide, axis=1, keepdims=True), (rows, LANES))
     scaled = (wide * gain).astype(BF16)
-    queries = (jnp.dot(scaled, wself[:, pl.ds(0, LANES)], preferred_element_type=F32) * self_scale).astype(BF16)
+    partial = jnp.dot(scaled, wself[...], preferred_element_type=F32)
+    for who in range(2):
+        s_p[:, pl.ds(512 * who, 384)] = partial[:, 384 * who : 384 * who + 384]
+        s_p[:, pl.ds(512 * who + 384, LANES)] = squares
+    pair_start(s_p.at[:, aligned(other_core, 512)], r_p, 9)
+    pair_wait(s_p.at[:, aligned(other_core, 512)], r_p, 9)
+    joined = s_p[:, aligned(core, 512)] + r_p[...]
+    self_scale = lax.rsqrt(joined[:, 384:] * (1.0 / d_model) + EPS)
+    queries = (joined[:, :LANES] * self_scale).astype(BF16)
 
     s_c[...] = queries
     g_c[aligned(b, rows), :] = queries
@@ -272,10 +276,9 @@
         lax.fori_loop(1, nb, step, 0)
 
     drains.append(drain_c)
-    projected = jnp.dot(scaled, wself[:, pl.ds(LANES, 2 * LANES)], preferred_element_type=F32) * self_scale
-    projected = projected.astype(BF16).astype(F32)
-    own_values = projected[:, LANES:]
-    products = queries.astype(F32) * projected[:, :LANES]
+    swap_start(3, 4, 5, 6, 7)
+    own_values = (joined[:, 2 * LANES : 3 * LANES] * self_scale).astype(BF16).astype(F32)
+    products = queries.astype(F32) * (joined[:, LANES : 2 * LANES] * self_scale).astype(BF16).astype(F32)
     low = lax.broadcasted_iota(jnp.int32, products.shape, 1) < 64
     own_0 = jnp.sum(jnp.where(low, products, 0.0), axis=1, keepdims=True) * score_scale
     own_1 = jnp.sum(jnp.where(low, 0.0, products), axis=1, keepdims=True) * score_scale
@@ -339,9 +342,7 @@
         lax.fori_loop(1, nb, step, 0)
 
     drains.append(drain_d)
-    swap_wait(0)
-    swap_wait(1)
-    ready(4)
+    swap_wait(3, 4)
 
     def wait_d(k, total):
         source = lax.rem(b + k, nb)
@@ -361,13 +362,12 @@
     attended = attended.astype(BF16)
     s_t[...] = attended
     g_t[:, aligned(core)] = attended
-    pair_start(s_t, g_t, 5)
-    pair_wait(s_t, g_t, 5)
+    pair_start(s_t, g_t.at[:, aligned(core)], 10)
+    pair_wait(s_t, g_t.at[:, aligned(other_core)], 10)
 
     s_e[...] = jnp.dot(g_t[...], wso[...], preferred_element_type=F32).astype(BF16)
     scatter_start(s_e, r_e, e_send, e_recv)
-    swap_wait(2)
-    swap_wait(3)
+    swap_wait(5, 6, 7)
 
     def turn(g, carry):
         vt_mem[aligned(g, 256), :] = values[:, aligned(g, 256)].T
@@ -380,9 +380,9 @@
 
     s_m[...] = middle_16
     g_m[:, aligned(core)] = middle_16
-    pair_start(s_m, g_m, 6)
-    pair_wait(s_x, g_x, 4)
-    pair_wait(s_m, g_m, 6)
+    pair_start(s_m, g_m.at[:, aligned(core)], 11)
+    pair_wait(s_x, g_x.at[:, aligned(other_core)], 8)
+    pair_wait(s_m, g_m.at[:, aligned(other_core)], 11)
     both_middle = g_m[...].astype(F32)
     cross_scaled = (both_middle * g_x[0:1, :]).astype(BF16)
     s_f[...] = jnp.dot(cross_scaled, wcq[...], preferred_element_type=F32).astype(BF16)
@@ -397,12 +397,8 @@
     s_q[pl.ds(0, rows), :] = raw
     g_q[pl.ds(0, rows), aligned(chip)] = raw
 
-    for k in steps:
-        remote(s_q, g_q.at[:, aligned(chip)], q_send.at[k], q_recv.at[chip], peer(k)).start()
-    drains.append(functools.partial(simple_drain, s_q, q_send))
-    for k in steps:
-        source = chip_at(half - k)
-        remote(s_q, g_q.at[:, aligned(source)], q_send.at[k], q_recv.at[source], (b, partner)).wait_recv()
+    gather_start(s_q, g_q, q_send, q_recv)
+    gather_wait(s_q, g_q, q_send, q_recv)
     sums = jnp.zeros((8, LANES), F32)
     for k in range(half):
         sums = sums + g_q[pl.ds(rows, 8), pl.ds(k * LANES, LANES)].astype(F32)
@@ -476,14 +472,20 @@
     crossed = jnp.concatenate([turned[rows * at : rows * at + rows] for at in (0, 2, 1, 3)], axis=1).astype(BF16)
 
     s_h[...] = crossed
-    g_h[:, aligned(c)] = crossed
+    g_h[:, aligned(chip)] = crossed
     gather_start(s_h, g_h, h_send, h_recv)
-    gather_pass(s_h, g_h, h_send, h_recv)
     gather_wait(s_h, g_h, h_send, h_recv)
-    out_ref[...] = (middle + jnp.dot(g_h[...], wco[...], preferred_element_type=F32)).astype(BF16)
+    s_o[...] = jnp.dot(g_h[...], wco[...], preferred_element_type=F32)
+    theirs = s_o.at[:, aligned(other_core)]
+    pair_start(theirs, r_o, 12)
+    pair_wait(theirs, r_o, 12)
+    result[...] = (middle + s_o[:, aligned(core)] + r_o[...]).astype(BF16)
+    leave = pltpu.make_async_copy(result, out_hbm, load_sem.at[14])
+    leave.start()
 
     for drain in drains:
         drain()
+    leave.wait()
 
 
 def body(
@@ -495,7 +497,6 @@
     cache_rows = cache_kv.shape[0] * cache_kv.shape[1] * cache_kv.shape[2]
     mem_count, mem_width = memory_kv.shape
     width = cache_rows // rows
-    vmem = pl.BlockSpec(memory_space=pltpu.VMEM)
     hbm = pl.BlockSpec(memory_space=pl.ANY)
     wide = nc * LANES
     chips = nc // 2
@@ -503,19 +504,23 @@
     def v(*shape):
         return pltpu.VMEM(shape, BF16)
 
+    def f(*shape):
+        return pltpu.VMEM(shape, F32)
+
     def sems(count):
         return pltpu.SemaphoreType.DMA((count,))
 
     return pl.pallas_call(
         functools.partial(kernel, nb, nc, d_model),
         out_shape=jax.ShapeDtypeStruct((rows, LANES), BF16),
-        in_specs=[vmem] * 5 + [hbm] * 6,
-        out_specs=vmem,
+        in_specs=[hbm] * 11,
+        out_specs=hbm,
         scratch_shapes=[
-            v(d_model, 3 * LANES), v(2 * LANES, wide // 2), v(2 * LANES, wide // 2), v(mem_width // 2, LANES),
+            v(1, LANES), v(1, LANES), pltpu.VMEM((1, hyps), jnp.int32), pltpu.VMEM((1, hyps), jnp.int32), v(rows, LANES),
+            v(d_model // 2, 6 * LANES), v(2 * LANES, wide // 2), v(2 * LANES, wide // 2), v(wide // 2, 2 * LANES),
             v(cache_rows, LANES), v(2 * mem_count, wide // 2), v(2 * mem_count, wide // 2), v(wide // 2, 2 * mem_count),
             v(width, rows * LANES), v(width, rows * LANES), v(hyps, rows * LANES), pltpu.VMEM((hyps, LANES), F32),
-            v(rows + 8, LANES), v(rows + 8, wide), pltpu.VMEM((8, LANES), F32), pltpu.VMEM((8, 2 * LANES), F32),
+            v(rows + 8, LANES), v(rows + 8, wide // 2), pltpu.VMEM((8, LANES), F32), pltpu.VMEM((8, 2 * LANES), F32),
             v(rows, LANES), v(hyps, LANES),
             v(hyps, 2 * LANES), v(nb, rows, 2 * LANES),
             v(rows, LANES), v(rows, 2 * LANES),
@@ -524,10 +529,11 @@
             v(rows, wide // 2), v(chips, rows, LANES),
             v(rows + 8, LANES), v(rows + 8, wide // 2),
             v(chips, 40, LANES), v(chips, 40, LANES),
-            v(rows, LANES), v(rows, wide),
-            sems(9), sems(7), sems(7),
-            sems(nc), sems(nc), sems(nb), sems(nb), sems(nb), sems(nb), sems(chips), sems(chips),
-            sems(chips), sems(chips), sems(chips), sems(chips), sems(chips), sems(chips), sems(nc), sems(nc),
+            v(rows, LANES), v(rows, wide // 2),
+            f(rows, 8 * LANES), f(rows, 4 * LANES), f(rows, 2 * LANES), f(rows, LANES),
+            sems(15), sems(13), sems(13),
+            sems(chips), sems(chips), sems(nb), sems(nb), sems(nb), sems(nb), sems(chips), sems(chips),
+            sems(chips), sems(chips), sems(chips), sems(chips), sems(chips), sems(chips), sems(chips), sems(chips),
         ],
         compiler_params=pltpu.CompilerParams(
             collective_id=0, has_side_effects=True, vmem_limit_bytes=VMEM_BYTES

time: 74.3 us -> 72.1 us (0.970)
  Pallas kernels: 72.8 us -> 70.6 us
    pallas_call x1, Pallas kernels: 72.8 us -> 70.6 us  [body(): pl.pallas_call(functools.partial(kernel, nb, nc, d_model), out_shape=jax....]
where the time goes in v3:
time: 72.1 us; the launch traced here: 71.9 us
  Pallas kernels  70.6 us (98%)
  local copies, waits for them, and re-layouts  1.3 us (2%)
    pallas_call x1, Pallas kernels, body(): pl.pallas_call(functools.partial(kernel, nb, nc, d_model), out_shape=jax....  70.6 us

profile of v3, /device:TPU:1, one launch (start us, length us, event | category | flops | bytes accessed | tf_op | source)
XLA Modules:
  0.0 71.9 jit_solution(14920993050910638429)
XLA Ops:
  0.0 70.6 %shard_map.109 = bf16[32,128]{1,0:T(8,128)(2,1)} custom-call(bf16[32,128]{1,0:T(8,128)(2,1)} %hid_hbm.1, bf16[1,128]{1,0:T(2,128)(2,1)} %bitcast.10, bf16[1,128]{1,0:T(2,128)(2,1)} %bitcast.11, s32[1,256]{1,0:T(1,128)} %bitcast.8, s32[1,256]{1,0:T(1,128)} %bitcast.9, bf16[3,4096,128]{2,1,0:T(8,128)(2,1)} %bitcast.6, bf16[128,4096]{1,0:T(8,128)(2,1)} %wso_hbm.1, ...), custom_call_target="tpu_custom_call" | custom-call | tf_op jit(solution)/shard_map/pallas_call | solution.py:513
  70.6 1.3 %copy.13 = bf16[32,128]{1,0:T(8,128)(2,1)} copy(bf16[32,128]{1,0:T(8,128)(2,1)} %shard_map.109) | data formatting | bytes 16384

commit v4 on v3

--- a/solution.py
+++ b/solution.py
@@ -14,6 +14,7 @@
 EPS = 1e-06
 LANES = 128
 VMEM_BYTES = 64000000
+AT_ONCE = 2
 
 
 def aligned(block, size=LANES):
@@ -183,18 +184,21 @@
 
     def gather_start(src, dst, send, recv):
         for k in steps:
-            remote(src, dst.at[:, aligned(chip)], send.at[k], recv.at[chip], peer(k)).start()
+            remote(src, dst.at[chip], send.at[k], recv.at[chip], peer(k)).start()
         drains.append(functools.partial(simple_drain, src, send))
 
     def gather_wait(src, dst, send, recv):
         for k in steps:
             source = chip_at(half - k)
-            remote(src, dst.at[:, aligned(source)], send.at[k], recv.at[source], (b, partner)).wait_recv()
+            remote(src, dst.at[source], send.at[k], recv.at[source], (b, partner)).wait_recv()
+
+    def gathered(dst):
+        return jnp.concatenate([dst[at, pl.ds(0, rows), :] for at in range(half)], axis=1)
 
     def scatter_start(src, dst, send, recv):
         for k in steps:
-            remote(src.at[:, aligned(chip_at(k))], dst.at[chip], send.at[k], recv.at[chip], peer(k)).start()
-        drains.append(functools.partial(simple_drain, src.at[:, aligned(chip)], send))
+            remote(src.at[chip_at(k)], dst.at[chip], send.at[k], recv.at[chip], peer(k)).start()
+        drains.append(functools.partial(simple_drain, src.at[chip], send))
 
     def simple_drain(block, send):
         def step(k, carry):
@@ -203,11 +207,15 @@
 
         lax.fori_loop(1, half, step, 0)
 
+    def scatter_fill(src, terms):
+        for at in range(half):
+            src[at] = terms[:, at * LANES : at * LANES + LANES].astype(BF16)
+
     def scatter_sum(src, dst, send, recv):
-        total = src[:, aligned(chip)].astype(F32)
+        total = src[chip].astype(F32)
         for k in steps:
             source = chip_at(half - k)
-            remote(src.at[:, aligned(chip)], dst.at[source], send.at[k], recv.at[source], (b, partner)).wait_recv()
+            remote(src.at[chip], dst.at[source], send.at[k], recv.at[source], (b, partner)).wait_recv()
             total = total + dst[source].astype(F32)
         return total
 
@@ -215,8 +223,8 @@
     first = s_a[pl.ds(0, rows), :]
     gain_rows = jnp.broadcast_to(sgain[...].astype(F32), (8, LANES)).astype(BF16)
     s_a[pl.ds(rows, 8), :] = gain_rows
-    g_a[pl.ds(0, rows), aligned(chip)] = first
-    g_a[pl.ds(rows, 8), aligned(chip)] = gain_rows
+    g_a[chip, pl.ds(0, rows), :] = first
+    g_a[chip, pl.ds(rows, 8), :] = gain_rows
     cgain_rows = jnp.broadcast_to(cgain[...].astype(F32), (8, LANES))
     s_x[...] = cgain_rows
     g_x[:, aligned(core)] = cgain_rows
@@ -244,18 +252,17 @@
     swap_wait(0, 1, 2)
     gather_wait(s_a, g_a, a_send, a_recv)
 
-    wide = g_a[pl.ds(0, rows), :].astype(F32)
-    gain = g_a[pl.ds(rows, 8), :].astype(F32)[0:1, :]
+    wide = gathered(g_a).astype(F32)
+    gain = jnp.concatenate([g_a[at, pl.ds(rows, 8), :] for at in range(half)], axis=1).astype(F32)[0:1, :]
     squares = jnp.broadcast_to(jnp.sum(wide * wide, axis=1, keepdims=True), (rows, LANES))
     scaled = (wide * gain).astype(BF16)
-    partial = jnp.dot(scaled, wself[...], preferred_element_type=F32)
-    for who in range(2):
-        s_p[:, pl.ds(512 * who, 384)] = partial[:, 384 * who : 384 * who + 384]
-        s_p[:, pl.ds(512 * who + 384, LANES)] = squares
-    pair_start(s_p.at[:, aligned(other_core, 512)], r_p, 9)
-    pair_wait(s_p.at[:, aligned(other_core, 512)], r_p, 9)
-    joined = s_p[:, aligned(core, 512)] + r_p[...]
-    self_scale = lax.rsqrt(joined[:, 384:] * (1.0 / d_model) + EPS)
+    s_p[:, pl.ds(0, 384)] = jnp.dot(scaled, wself[:, aligned(other_core, 384)], preferred_element_type=F32)
+    s_p[:, pl.ds(384, LANES)] = squares
+    pair_start(s_p, r_p, 9)
+    mine = jnp.dot(scaled, wself[:, aligned(core, 384)], preferred_element_type=F32)
+    pair_wait(s_p, r_p, 9)
+    joined = mine + r_p[:, pl.ds(0, 384)]
+    self_scale = lax.rsqrt((squares + r_p[:, pl.ds(384, LANES)]) * (1.0 / d_model) + EPS)
     queries = (joined[:, :LANES] * self_scale).astype(BF16)
 
     s_c[...] = queries
@@ -290,13 +297,11 @@
 
     lax.fori_loop(1, nb, wait_c, 0)
 
-    all_queries = g_c[...].astype(F32)
-
-    def spread_q(r, carry):
-        lhs_q[:, aligned(r)] = jnp.where(local_wide == r, all_queries, 0.0).astype(BF16)
-        return carry
-
-    lax.fori_loop(0, rows, spread_q, 0)
+    all_queries = g_c[...]
+    nothing = jnp.zeros(all_queries.shape, BF16)
+    local_16 = local_wide.astype(F32).astype(BF16)
+    for r in range(rows):
+        lhs_q[:, pl.ds(r * LANES, LANES)] = jnp.where(local_16 == r, all_queries, nothing)
     scores = lax.dot_general(lhs_q[...], kt[...], NT, preferred_element_type=F32) * score_scale
     lane = lax.broadcasted_iota(jnp.int32, scores.shape, 1)
     even = lax.rem(lane, 2) == 0
@@ -310,15 +315,12 @@
     weights = weights.astype(F32)
     total_0 = jnp.sum(jnp.where(even, weights, 0.0), axis=1, keepdims=True)
     total_1 = jnp.sum(jnp.where(even, 0.0, weights), axis=1, keepdims=True)
+    weights = lhs_q[:, pl.ds(0, width)]
     acc[...] = jnp.zeros(acc.shape, F32)
-
-    def select(r, carry):
-        both = jnp.dot(lhs_q[:, pl.ds(0, width)], vt[:, aligned(r, 2 * LANES)], preferred_element_type=F32)
-        picked = jnp.where(local_wide == 2 * r, both[:, :LANES], acc[...])
-        acc[...] = jnp.where(local_wide == 2 * r + 1, both[:, LANES:], picked)
-        return carry
-
-    lax.fori_loop(0, rows // 2, select, 0)
+    for r in range(0, rows, 2):
+        both = jnp.dot(weights, vt[:, pl.ds(r * LANES, 2 * LANES)], preferred_element_type=F32)
+        picked = jnp.where(local_wide == r, both[:, :LANES], acc[...])
+        acc[...] = jnp.where(local_wide == r + 1, both[:, LANES:], picked)
     summed = acc[...]
     lane = lax.broadcasted_iota(jnp.int32, summed.shape, 1)
     here = (local_wide >= 0) & (local_wide < rows)
@@ -363,9 +365,11 @@
     s_t[...] = attended
     g_t[:, aligned(core)] = attended
     pair_start(s_t, g_t.at[:, aligned(core)], 10)
+
+    terms = jnp.dot(attended, wso[aligned(core), :], preferred_element_type=F32)
     pair_wait(s_t, g_t.at[:, aligned(other_core)], 10)
-
-    s_e[...] = jnp.dot(g_t[...], wso[...], preferred_element_type=F32).astype(BF16)
+    terms = terms + jnp.dot(g_t[:, aligned(other_core)], wso[aligned(other_core), :], preferred_element_type=F32)
+    scatter_fill(s_e, terms)
     scatter_start(s_e, r_e, e_send, e_recv)
     swap_wait(5, 6, 7)
 
@@ -385,23 +389,23 @@
     pair_wait(s_m, g_m.at[:, aligned(other_core)], 11)
     both_middle = g_m[...].astype(F32)
     cross_scaled = (both_middle * g_x[0:1, :]).astype(BF16)
-    s_f[...] = jnp.dot(cross_scaled, wcq[...], preferred_element_type=F32).astype(BF16)
+    scatter_fill(s_f, jnp.dot(cross_scaled, wcq[...], preferred_element_type=F32))
     scatter_start(s_f, r_f, f_send, f_recv)
     squares = jnp.broadcast_to(jnp.sum(both_middle * both_middle, axis=1, keepdims=True), (rows, LANES))
     squares = jnp.concatenate([squares] * (LANES // rows), axis=0).T[0:1, :]
     row8 = lax.broadcasted_iota(jnp.int32, (8, LANES), 0)
     square_rows = place(row8, split3(squares)).astype(BF16)
     s_q[pl.ds(rows, 8), :] = square_rows
-    g_q[pl.ds(rows, 8), aligned(chip)] = square_rows
+    g_q[chip, pl.ds(rows, 8), :] = square_rows
     raw = scatter_sum(s_f, r_f, f_send, f_recv).astype(BF16)
     s_q[pl.ds(0, rows), :] = raw
-    g_q[pl.ds(0, rows), aligned(chip)] = raw
+    g_q[chip, pl.ds(0, rows), :] = raw
 
     gather_start(s_q, g_q, q_send, q_recv)
     gather_wait(s_q, g_q, q_send, q_recv)
     sums = jnp.zeros((8, LANES), F32)
     for k in range(half):
-        sums = sums + g_q[pl.ds(rows, 8), pl.ds(k * LANES, LANES)].astype(F32)
+        sums = sums + g_q[k, pl.ds(rows, 8), :].astype(F32)
     mean = (sums[0:1, :] + sums[1:2, :] + sums[2:3, :]) * (1.0 / d_model)
     factor = lax.rsqrt(mean + EPS) * score_scale
 
@@ -412,21 +416,11 @@
     lane_head = lax.div(lax.broadcasted_iota(jnp.int32, (64, LANES), 1), rows)
     left = lax.broadcasted_iota(jnp.int32, (32, LANES), 1) < 64
 
-    def deliver(g):
-        for which in range(2):
-            target = 2 * g + which
-
-            @pl.when(target != chip)
-            def _():
-                remote(
-                    s_g.at[target], r_g.at[chip], g_send.at[target], g_recv.at[chip], (b, 2 * target + core)
-                ).start()
-
-    offsets = sorted(range(groups), key=lambda k: -min(k % 4, 4 - k % 4) if k else 1)
-    previous = None
-    for offset in offsets:
-        g = lax.rem(lax.div(chip, 2) + offset, groups)
-        query = g_q[pl.ds(0, rows), aligned(g, 256)].astype(F32)
+    def deliver(target):
+        remote(s_g.at[target], r_g.at[chip], g_send.at[target], g_recv.at[chip], (b, 2 * target + core)).start()
+
+    def remember(g):
+        query = jnp.concatenate([g_q[2 * g, pl.ds(0, rows), :], g_q[2 * g + 1, pl.ds(0, rows), :]], axis=1).astype(F32)
         query = jnp.where(own_block, jnp.concatenate([query] * 4, axis=0), 0.0).astype(BF16)
         score = lax.dot_general(keys[:, aligned(g, 256)], query, NT, preferred_element_type=F32) * factor
         most = jnp.max(score, axis=0, keepdims=True)
@@ -443,10 +437,22 @@
         s_g[2 * g, pl.ds(32, 8), :] = jnp.where(left[0:8], stat, turned_stat).astype(BF16)
         s_g[2 * g + 1, pl.ds(0, 32), :] = jnp.where(left, turned[0:32], taken[32:64]).astype(BF16)
         s_g[2 * g + 1, pl.ds(32, 8), :] = jnp.where(left[0:8], turned_stat, stat).astype(BF16)
-        if previous is not None:
-            deliver(previous)
-        previous = g
-    deliver(previous)
+
+    own_group = lax.div(chip, 2)
+    offsets = sorted(range(groups), key=lambda k: -min(k % 4, 4 - k % 4) if k else 1)
+    waiting = []
+    for first_at in range(0, groups, AT_ONCE):
+        now = offsets[first_at : first_at + AT_ONCE]
+        for offset in now:
+            remember(lax.rem(own_group + offset, groups))
+        for target in waiting:
+            deliver(target)
+        waiting = []
+        for offset in now:
+            g = lax.rem(own_group + offset, groups)
+            waiting += [2 * g, 2 * g + 1] if offset else [chip + 1 - 2 * lax.rem(chip, 2)]
+    for target in waiting:
+        deliver(target)
     r_g[chip] = s_g[chip]
 
     def drain_g():
@@ -472,14 +478,15 @@
     crossed = jnp.concatenate([turned[rows * at : rows * at + rows] for at in (0, 2, 1, 3)], axis=1).astype(BF16)
 
     s_h[...] = crossed
-    g_h[:, aligned(chip)] = crossed
+    g_h[chip] = crossed
     gather_start(s_h, g_h, h_send, h_recv)
     gather_wait(s_h, g_h, h_send, h_recv)
-    s_o[...] = jnp.dot(g_h[...], wco[...], preferred_element_type=F32)
-    theirs = s_o.at[:, aligned(other_core)]
-    pair_start(theirs, r_o, 12)
-    pair_wait(theirs, r_o, 12)
-    result[...] = (middle + s_o[:, aligned(core)] + r_o[...]).astype(BF16)
+    everything = gathered(g_h)
+    s_o[...] = jnp.dot(everything, wco[:, aligned(other_core)], preferred_element_type=F32)
+    pair_start(s_o, r_o, 12)
+    mine = middle + jnp.dot(everything, wco[:, aligned(core)], preferred_element_type=F32)
+    pair_wait(s_o, r_o, 12)
+    result[...] = (mine + r_o[...]).astype(BF16)
     leave = pltpu.make_async_copy(result, out_hbm, load_sem.at[14])
     leave.start()
 
@@ -520,17 +527,17 @@
             v(d_model // 2, 6 * LANES), v(2 * LANES, wide // 2), v(2 * LANES, wide // 2), v(wide // 2, 2 * LANES),
             v(cache_rows, LANES), v(2 * mem_count, wide // 2), v(2 * mem_count, wide // 2), v(wide // 2, 2 * mem_count),
             v(width, rows * LANES), v(width, rows * LANES), v(hyps, rows * LANES), pltpu.VMEM((hyps, LANES), F32),
-            v(rows + 8, LANES), v(rows + 8, wide // 2), pltpu.VMEM((8, LANES), F32), pltpu.VMEM((8, 2 * LANES), F32),
+            v(rows + 8, LANES), v(chips, rows + 8, LANES), pltpu.VMEM((8, LANES), F32), pltpu.VMEM((8, 2 * LANES), F32),
             v(rows, LANES), v(hyps, LANES),
             v(hyps, 2 * LANES), v(nb, rows, 2 * LANES),
             v(rows, LANES), v(rows, 2 * LANES),
-            v(rows, wide // 2), v(chips, rows, LANES),
+            v(chips, rows, LANES), v(chips, rows, LANES),
             v(rows, LANES), v(rows, 2 * LANES),
-            v(rows, wide // 2), v(chips, rows, LANES),
-            v(rows + 8, LANES), v(rows + 8, wide // 2),
+            v(chips, rows, LANES), v(chips, rows, LANES),
+            v(rows + 8, LANES), v(chips, rows + 8, LANES),
             v(chips, 40, LANES), v(chips, 40, LANES),
-            v(rows, LANES), v(rows, wide // 2),
-            f(rows, 8 * LANES), f(rows, 4 * LANES), f(rows, 2 * LANES), f(rows, LANES),
+            v(rows, LANES), v(chips, rows, LANES),
+            f(rows, 4 * LANES), f(rows, 4 * LANES), f(rows, LANES), f(rows, LANES),
             sems(15), sems(13), sems(13),
             sems(chips), sems(chips), sems(nb), sems(nb), sems(nb), sems(nb), sems(chips), sems(chips),
             sems(chips), sems(chips), sems(chips), sems(chips), sems(chips), sems(chips), sems(chips), sems(chips),

time: 72.1 us -> 68.9 us (0.956)
  Pallas kernels: 70.6 us -> 67.4 us
    pallas_call x1, Pallas kernels: 70.6 us -> 67.4 us  [body(): pl.pallas_call(functools.partial(kernel, nb, nc, d_model), out_shape=jax....]
where the time goes in v4:
time: 68.9 us; the launch traced here: 68.7 us
  Pallas kernels  67.4 us (98%)
  local copies, waits for them, and re-layouts  1.3 us (2%)
    pallas_call x1, Pallas kernels, body(): pl.pallas_call(functools.partial(kernel, nb, nc, d_model), out_shape=jax....  67.4 us

profile of v4, /device:TPU:1, one launch (start us, length us, event | category | flops | bytes accessed | tf_op | source)
XLA Modules:
  0.0 68.7 jit_solution(14766471057116004122)
XLA Ops:
  0.0 67.4 %shard_map.109 = bf16[32,128]{1,0:T(8,128)(2,1)} custom-call(bf16[32,128]{1,0:T(8,128)(2,1)} %hid_hbm.1, bf16[1,128]{1,0:T(2,128)(2,1)} %bitcast.10, bf16[1,128]{1,0:T(2,128)(2,1)} %bitcast.11, s32[1,256]{1,0:T(1,128)} %bitcast.8, s32[1,256]{1,0:T(1,128)} %bitcast.9, bf16[3,4096,128]{2,1,0:T(8,128)(2,1)} %bitcast.6, bf16[128,4096]{1,0:T(8,128)(2,1)} %wso_hbm.1, ...), custom_call_target="tpu_custom_call" | custom-call | tf_op jit(solution)/shard_map/pallas_call | solution.py:520
  67.4 1.3 %copy.13 = bf16[32,128]{1,0:T(8,128)(2,1)} copy(bf16[32,128]{1,0:T(8,128)(2,1)} %shard_map.109) | data formatting | bytes 16384

commit v5 on v4

--- a/solution.py
+++ b/solution.py
@@ -42,8 +42,8 @@
     nb, nc, d_model,
     hid_hbm, sgain_hbm, cgain_hbm, parents_hbm, plen_hbm,
     wself_hbm, wso_hbm, wcq_hbm, wco_hbm, cache_hbm, mem_hbm,
-    out_hbm,
-    sgain, cgain, parents, plen, result,
+    out_ref,
+    sgain, cgain, parents, plen,
     wself, wso, wcq, wco, cache, keys, values, vt_mem, kt, vt, lhs_q, acc,
     s_a, g_a, s_x, g_x, s_c, g_c, s_d, r_d, s_t, g_t, s_e, r_e, s_m, g_m, s_f, r_f, s_q, g_q, s_g, r_g, s_h, g_h, s_p, r_p, s_o, r_o,
     load_sem, swap_send, swap_recv,
@@ -63,7 +63,15 @@
     core = lax.rem(c, 2)
     partner = c + 1 - 2 * core
     other_core = 1 - core
-    steps = sorted(range(1, half), key=lambda k: -min(k % 8, 8 - k % 8))
+    def hops(k):
+        return min(k % 8, 8 - k % 8)
+
+    def slot(k):
+        return (k + 2) % half
+
+    steps = sorted(range(1, half), key=lambda k: -hops(k))
+    far = sorted(slot(k) for k in range(half) if hops(k) >= 3)
+    near = [at for at in range(half) if at not in far]
 
     barrier = pltpu.get_barrier_semaphore()
 
@@ -100,34 +108,35 @@
             loads[at].wait()
             loaded.add(at)
 
-    def columns(source, target, offset=0):
+    def columns(source, target, offset=0, absolute=False):
         height = source.shape[0]
         return (
             lambda g, side: source.at[:, aligned(offset + 2 * g + side)],
-            lambda g, who: target.at[aligned(who, height), aligned(g)],
+            lambda k, g, who: target.at[aligned(who, height), aligned(g if absolute else k)],
             lambda who: target.at[aligned(who, height), :],
         )
 
     def kind(which):
         return (
             lambda g, side: wself_hbm.at[which, aligned(2 * g + side), :],
-            lambda g, who: wself.at[aligned(g), aligned(3 * who + which)],
+            lambda k, g, who: wself.at[aligned(k), aligned(3 * who + which)],
             lambda who: wself.at[:, aligned(3 * who + which)],
         )
 
     out_rows = (
         lambda g, side: wco_hbm.at[aligned(2 * g + side), :],
-        lambda g, who: wco.at[aligned(g), aligned(who)],
+        lambda k, g, who: wco.at[aligned(k), aligned(who)],
         lambda who: wco.at[:, aligned(who)],
     )
     shared = [
         kind(0), kind(1), kind(2), columns(wso_hbm, wso), columns(wcq_hbm, wcq),
-        columns(mem_hbm, keys), columns(mem_hbm, values, nc), out_rows,
+        columns(mem_hbm, keys, 0, True), columns(mem_hbm, values, nc, True), out_rows,
     ]
 
-    def keep(g, carry):
+    def keep(k, carry):
+        g, at_slot = lax.rem(chip + k, half), lax.rem(k + 2, half)
         for at, (block, place_at, whole) in enumerate(shared):
-            pltpu.make_async_copy(block(g, core), place_at(g, core), load_sem.at[6 + at]).start()
+            pltpu.make_async_copy(block(g, core), place_at(at_slot, g, core), load_sem.at[6 + at]).start()
         return carry
 
     lax.fori_loop(0, half, keep, 0)
@@ -144,11 +153,12 @@
         return lax.rem(chip + k, half)
 
     def swap_start(*which):
-        def step(g, carry):
+        def step(k, carry):
+            g, at_slot = lax.rem(chip + k, half), lax.rem(k + 2, half)
             for at in which:
                 block, place_at, whole = shared[at]
                 remote(
-                    block(g, other_core), place_at(g, core), swap_send.at[at], swap_recv.at[at], (b, partner)
+                    block(g, other_core), place_at(at_slot, g, core), swap_send.at[at], swap_recv.at[at], (b, partner)
                 ).start()
             return carry
 
@@ -184,21 +194,37 @@
 
     def gather_start(src, dst, send, recv):
         for k in steps:
-            remote(src, dst.at[chip], send.at[k], recv.at[chip], peer(k)).start()
+            remote(src, dst.at[slot(half - k)], send.at[k], recv.at[slot(half - k)], peer(k)).start()
         drains.append(functools.partial(simple_drain, src, send))
 
-    def gather_wait(src, dst, send, recv):
+    def gather_wait(src, dst, send, recv, which):
+        for k in reversed(steps):
+            at = slot(half - k)
+            if at in which:
+                remote(src, dst.at[at], send.at[k], recv.at[at], (b, partner)).wait_recv()
+
+    def scatter_send(src, dst, send, recv, which):
         for k in steps:
-            source = chip_at(half - k)
-            remote(src, dst.at[source], send.at[k], recv.at[source], (b, partner)).wait_recv()
-
-    def gathered(dst):
-        return jnp.concatenate([dst[at, pl.ds(0, rows), :] for at in range(half)], axis=1)
-
-    def scatter_start(src, dst, send, recv):
-        for k in steps:
-            remote(src.at[chip_at(k)], dst.at[chip], send.at[k], recv.at[chip], peer(k)).start()
-        drains.append(functools.partial(simple_drain, src.at[chip], send))
+            if slot(k) in which:
+                remote(
+                    src.at[slot(k)], dst.at[slot(half - k)], send.at[k], recv.at[slot(half - k)], peer(k)
+                ).start()
+
+    def scatter_products(products, src, dst, send, recv):
+        before = None
+        for which in (far, near):
+            if which:
+                terms = products(which)
+                for at, which_slot in enumerate(which):
+                    src[which_slot] = terms[:, at * LANES : at * LANES + LANES].astype(BF16)
+                if before:
+                    scatter_send(src, dst, send, recv, before)
+                before = which
+        scatter_send(src, dst, send, recv, before)
+        drains.append(functools.partial(simple_drain, src.at[0], send))
+
+    def taken_columns(ref, rows_at, which):
+        return jnp.concatenate([ref[rows_at, pl.ds(at * LANES, LANES)] for at in which], axis=1)
 
     def simple_drain(block, send):
         def step(k, carry):
@@ -207,24 +233,20 @@
 
         lax.fori_loop(1, half, step, 0)
 
-    def scatter_fill(src, terms):
-        for at in range(half):
-            src[at] = terms[:, at * LANES : at * LANES + LANES].astype(BF16)
-
     def scatter_sum(src, dst, send, recv):
-        total = src[chip].astype(F32)
-        for k in steps:
-            source = chip_at(half - k)
-            remote(src.at[chip], dst.at[source], send.at[k], recv.at[source], (b, partner)).wait_recv()
-            total = total + dst[source].astype(F32)
+        total = src[slot(0)].astype(F32)
+        for k in reversed(steps):
+            at = slot(half - k)
+            remote(src.at[at], dst.at[at], send.at[k], recv.at[at], (b, partner)).wait_recv()
+            total = total + dst[at].astype(F32)
         return total
 
     ready(0, 1, 2)
     first = s_a[pl.ds(0, rows), :]
     gain_rows = jnp.broadcast_to(sgain[...].astype(F32), (8, LANES)).astype(BF16)
     s_a[pl.ds(rows, 8), :] = gain_rows
-    g_a[chip, pl.ds(0, rows), :] = first
-    g_a[chip, pl.ds(rows, 8), :] = gain_rows
+    g_a[slot(0), pl.ds(0, rows), :] = first
+    g_a[slot(0), pl.ds(rows, 8), :] = gain_rows
     cgain_rows = jnp.broadcast_to(cgain[...].astype(F32), (8, LANES))
     s_x[...] = cgain_rows
     g_x[:, aligned(core)] = cgain_rows
@@ -250,16 +272,32 @@
     local_wide = jnp.broadcast_to(parents[...], (LANES, hyps)).T - b * rows
     plen_wide = jnp.broadcast_to(plen[...], (LANES, hyps)).T
     swap_wait(0, 1, 2)
-    gather_wait(s_a, g_a, a_send, a_recv)
-
-    wide = gathered(g_a).astype(F32)
-    gain = jnp.concatenate([g_a[at, pl.ds(rows, 8), :] for at in range(half)], axis=1).astype(F32)[0:1, :]
-    squares = jnp.broadcast_to(jnp.sum(wide * wide, axis=1, keepdims=True), (rows, LANES))
-    scaled = (wide * gain).astype(BF16)
-    s_p[:, pl.ds(0, 384)] = jnp.dot(scaled, wself[:, aligned(other_core, 384)], preferred_element_type=F32)
+
+    def project(which):
+        wide = jnp.concatenate([g_a[at, pl.ds(0, rows), :] for at in which], axis=1).astype(F32)
+        gain = jnp.concatenate([g_a[at, pl.ds(rows, 8), :] for at in which], axis=1).astype(F32)[0:1, :]
+        scaled = (wide * gain).astype(BF16)
+
+        def columns_of(who):
+            weight = jnp.concatenate([wself[pl.ds(at * LANES, LANES), aligned(who, 384)] for at in which], axis=0)
+            return jnp.dot(scaled, weight, preferred_element_type=F32)
+
+        return jnp.sum(wide * wide, axis=1, keepdims=True), columns_of
+
+    gather_wait(s_a, g_a, a_send, a_recv, near)
+    squares, columns_of = project(near)
+    theirs, mine = columns_of(other_core), columns_of(core)
+    gather_wait(s_a, g_a, a_send, a_recv, far)
+    if far:
+        far_squares, columns_of = project(far)
+        squares = squares + far_squares
+        theirs = theirs + columns_of(other_core)
+    squares = jnp.broadcast_to(squares, (rows, LANES))
+    s_p[:, pl.ds(0, 384)] = theirs
     s_p[:, pl.ds(384, LANES)] = squares
     pair_start(s_p, r_p, 9)
-    mine = jnp.dot(scaled, wself[:, aligned(core, 384)], preferred_element_type=F32)
+    if far:
+        mine = mine + columns_of(core)
     pair_wait(s_p, r_p, 9)
     joined = mine + r_p[:, pl.ds(0, 384)]
     self_scale = lax.rsqrt((squares + r_p[:, pl.ds(384, LANES)]) * (1.0 / d_model) + EPS)
@@ -366,11 +404,17 @@
     g_t[:, aligned(core)] = attended
     pair_start(s_t, g_t.at[:, aligned(core)], 10)
 
-    terms = jnp.dot(attended, wso[aligned(core), :], preferred_element_type=F32)
+    mine = {
+        len(which): jnp.dot(attended, taken_columns(wso, aligned(core), which), preferred_element_type=F32)
+        for which in (far, near) if which
+    }
     pair_wait(s_t, g_t.at[:, aligned(other_core)], 10)
-    terms = terms + jnp.dot(g_t[:, aligned(other_core)], wso[aligned(other_core), :], preferred_element_type=F32)
-    scatter_fill(s_e, terms)
-    scatter_start(s_e, r_e, e_send, e_recv)
+    theirs = g_t[:, aligned(other_core)]
+    scatter_products(
+        lambda which: mine[len(which)]
+        + jnp.dot(theirs, taken_columns(wso, aligned(other_core), which), preferred_element_type=F32),
+        s_e, r_e, e_send, e_recv,
+    )
     swap_wait(5, 6, 7)
 
     def turn(g, carry):
@@ -389,20 +433,22 @@
     pair_wait(s_m, g_m.at[:, aligned(other_core)], 11)
     both_middle = g_m[...].astype(F32)
     cross_scaled = (both_middle * g_x[0:1, :]).astype(BF16)
-    scatter_fill(s_f, jnp.dot(cross_scaled, wcq[...], preferred_element_type=F32))
-    scatter_start(s_f, r_f, f_send, f_recv)
+    scatter_products(
+        lambda which: jnp.dot(cross_scaled, taken_columns(wcq, slice(None), which), preferred_element_type=F32),
+        s_f, r_f, f_send, f_recv,
+    )
     squares = jnp.broadcast_to(jnp.sum(both_middle * both_middle, axis=1, keepdims=True), (rows, LANES))
     squares = jnp.concatenate([squares] * (LANES // rows), axis=0).T[0:1, :]
     row8 = lax.broadcasted_iota(jnp.int32, (8, LANES), 0)
     square_rows = place(row8, split3(squares)).astype(BF16)
     s_q[pl.ds(rows, 8), :] = square_rows
-    g_q[chip, pl.ds(rows, 8), :] = square_rows
+    g_q[slot(0), pl.ds(rows, 8), :] = square_rows
     raw = scatter_sum(s_f, r_f, f_send, f_recv).astype(BF16)
     s_q[pl.ds(0, rows), :] = raw
-    g_q[chip, pl.ds(0, rows), :] = raw
+    g_q[slot(0), pl.ds(0, rows), :] = raw
 
     gather_start(s_q, g_q, q_send, q_recv)
-    gather_wait(s_q, g_q, q_send, q_recv)
+    gather_wait(s_q, g_q, q_send, q_recv, far + near)
     sums = jnp.zeros((8, LANES), F32)
     for k in range(half):
         sums = sums + g_q[k, pl.ds(rows, 8), :].astype(F32)
@@ -420,7 +466,9 @@
         remote(s_g.at[target], r_g.at[chip], g_send.at[target], g_recv.at[chip], (b, 2 * target + core)).start()
 
     def remember(g):
-        query = jnp.concatenate([g_q[2 * g, pl.ds(0, rows), :], g_q[2 * g + 1, pl.ds(0, rows), :]], axis=1).astype(F32)
+        query = jnp.concatenate(
+            [g_q[lax.rem(2 * g + which - chip + half + 2, half), pl.ds(0, rows), :] for which in range(2)], axis=1
+        ).astype(F32)
         query = jnp.where(own_block, jnp.concatenate([query] * 4, axis=0), 0.0).astype(BF16)
         score = lax.dot_general(keys[:, aligned(g, 256)], query, NT, preferred_element_type=F32) * factor
         most = jnp.max(score, axis=0, keepdims=True)
@@ -478,21 +526,28 @@
     crossed = jnp.concatenate([turned[rows * at : rows * at + rows] for at in (0, 2, 1, 3)], axis=1).astype(BF16)
 
     s_h[...] = crossed
-    g_h[chip] = crossed
+    g_h[slot(0)] = crossed
     gather_start(s_h, g_h, h_send, h_recv)
-    gather_wait(s_h, g_h, h_send, h_recv)
-    everything = gathered(g_h)
-    s_o[...] = jnp.dot(everything, wco[:, aligned(other_core)], preferred_element_type=F32)
+
+    def products(which, who):
+        block = jnp.concatenate([g_h[at] for at in which], axis=1)
+        weight = jnp.concatenate([wco[pl.ds(at * LANES, LANES), aligned(who)] for at in which], axis=0)
+        return jnp.dot(block, weight, preferred_element_type=F32)
+
+    gather_wait(s_h, g_h, h_send, h_recv, near)
+    theirs, mine = products(near, other_core), middle + products(near, core)
+    gather_wait(s_h, g_h, h_send, h_recv, far)
+    if far:
+        theirs = theirs + products(far, other_core)
+    s_o[...] = theirs
     pair_start(s_o, r_o, 12)
-    mine = middle + jnp.dot(everything, wco[:, aligned(core)], preferred_element_type=F32)
+    if far:
+        mine = mine + products(far, core)
     pair_wait(s_o, r_o, 12)
-    result[...] = (mine + r_o[...]).astype(BF16)
-    leave = pltpu.make_async_copy(result, out_hbm, load_sem.at[14])
-    leave.start()
+    out_ref[...] = (mine + r_o[...]).astype(BF16)
 
     for drain in drains:
         drain()
-    leave.wait()
 
 
 def body(
@@ -519,11 +574,11 @@
 
     return pl.pallas_call(
         functools.partial(kernel, nb, nc, d_model),
-        out_shape=jax.ShapeDtypeStruct((rows, LANES), BF16),
+        out_shape=pltpu.VMEM((rows, LANES), BF16),
         in_specs=[hbm] * 11,
-        out_specs=hbm,
+        out_specs=pl.BlockSpec(memory_space=pltpu.VMEM),
         scratch_shapes=[
-            v(1, LANES), v(1, LANES), pltpu.VMEM((1, hyps), jnp.int32), pltpu.VMEM((1, hyps), jnp.int32), v(rows, LANES),
+            v(1, LANES), v(1, LANES), pltpu.VMEM((1, hyps), jnp.int32), pltpu.VMEM((1, hyps), jnp.int32),
             v(d_model // 2, 6 * LANES), v(2 * LANES, wide // 2), v(2 * LANES, wide // 2), v(wide // 2, 2 * LANES),
             v(cache_rows, LANES), v(2 * mem_count, wide // 2), v(2 * mem_count, wide // 2), v(wide // 2, 2 * mem_count),
             v(width, rows * LANES), v(width, rows * LANES), v(hyps, rows * LANES), pltpu.VMEM((hyps, LANES), F32),

time: 68.9 us -> 67.8 us (0.984)
  local copies, waits for them, and re-layouts: 1.3 us -> 0.6 us
    unnamed x1, local copies, waits for them, and re-layouts: 1.3 us -> 0.6 us
where the time goes in v5:
time: 67.8 us; the launch traced here: 67.7 us
  Pallas kernels  67.1 us (99%)
    pallas_call x1, Pallas kernels, body(): pl.pallas_call(functools.partial(kernel, nb, nc, d_model), out_shape=pltp...  67.1 us

profile of v5, /device:TPU:1, one launch (start us, length us, event | category | flops | bytes accessed | tf_op | source)
XLA Modules:
  0.0 67.7 jit_solution(9392730354748030326)
XLA Ops:
  0.0 67.1 %shard_map.109 = bf16[32,128]{1,0:T(8,128)(2,1)S(1)} custom-call(bf16[32,128]{1,0:T(8,128)(2,1)} %hid_hbm.1, bf16[1,128]{1,0:T(2,128)(2,1)} %bitcast.10, bf16[1,128]{1,0:T(2,128)(2,1)} %bitcast.11, s32[1,256]{1,0:T(1,128)} %bitcast.8, s32[1,256]{1,0:T(1,128)} %bitcast.9, bf16[3,4096,128]{2,1,0:T(8,128)(2,1)} %bitcast.6, bf16[128,4096]{1,0:T(8,128)(2,1)} %wso_hbm.1, ...), custom_call_target="tpu_custom_call" | custom-call | tf_op jit(solution)/shard_map/pallas_call | solution.py:575
  67.1 0.6 copy.13

commit v6 on v5

--- a/solution.py
+++ b/solution.py
@@ -45,10 +45,10 @@
     out_ref,
     sgain, cgain, parents, plen,
     wself, wso, wcq, wco, cache, keys, values, vt_mem, kt, vt, lhs_q, acc,
-    s_a, g_a, s_x, g_x, s_c, g_c, s_d, r_d, s_t, g_t, s_e, r_e, s_m, g_m, s_f, r_f, s_q, g_q, s_g, r_g, s_h, g_h, s_p, r_p, s_o, r_o,
+    s_a, g_a, s_x, g_x, s_c, g_c, s_d, r_d, s_t, g_t, s_e, r_e, s_m, g_m, s_f, r_f, s_q, g_q, s_g, r_g, s_h, g_h, s_p, r_p, s_o, r_o, s_n, g_n,
     load_sem, swap_send, swap_recv,
     a_send, a_recv, c_send, c_recv, d_send, d_recv, e_send, e_recv,
-    f_send, f_recv, q_send, q_recv, g_send, g_recv, h_send, h_recv,
+    f_send, f_recv, q_send, q_recv, g_send, g_recv, h_send, h_recv, n_send, n_recv,
 ):
     rows = hid_hbm.shape[0]
     hyps = nb * rows
@@ -441,17 +441,18 @@
     squares = jnp.concatenate([squares] * (LANES // rows), axis=0).T[0:1, :]
     row8 = lax.broadcasted_iota(jnp.int32, (8, LANES), 0)
     square_rows = place(row8, split3(squares)).astype(BF16)
-    s_q[pl.ds(rows, 8), :] = square_rows
-    g_q[slot(0), pl.ds(rows, 8), :] = square_rows
+    s_n[...] = square_rows
+    g_n[slot(0)] = square_rows
+    gather_start(s_n, g_n, n_send, n_recv)
     raw = scatter_sum(s_f, r_f, f_send, f_recv).astype(BF16)
-    s_q[pl.ds(0, rows), :] = raw
-    g_q[slot(0), pl.ds(0, rows), :] = raw
-
+
+    s_q[...] = raw
+    g_q[slot(0)] = raw
     gather_start(s_q, g_q, q_send, q_recv)
-    gather_wait(s_q, g_q, q_send, q_recv, far + near)
+    gather_wait(s_n, g_n, n_send, n_recv, far + near)
     sums = jnp.zeros((8, LANES), F32)
-    for k in range(half):
-        sums = sums + g_q[k, pl.ds(rows, 8), :].astype(F32)
+    for at in range(half):
+        sums = sums + g_n[at].astype(F32)
     mean = (sums[0:1, :] + sums[1:2, :] + sums[2:3, :]) * (1.0 / d_model)
     factor = lax.rsqrt(mean + EPS) * score_scale
 
@@ -465,10 +466,15 @@
     def deliver(target):
         remote(s_g.at[target], r_g.at[chip], g_send.at[target], g_recv.at[chip], (b, 2 * target + core)).start()
 
+    def slot_of(other):
+        return lax.rem(other - chip + half + 2, half)
+
+    def arrived(other):
+        at = slot_of(other)
+        remote(s_q, g_q.at[at], q_send.at[1], q_recv.at[at], (b, partner)).wait_recv()
+
     def remember(g):
-        query = jnp.concatenate(
-            [g_q[lax.rem(2 * g + which - chip + half + 2, half), pl.ds(0, rows), :] for which in range(2)], axis=1
-        ).astype(F32)
+        query = jnp.concatenate([g_q[slot_of(2 * g)], g_q[slot_of(2 * g + 1)]], axis=1).astype(F32)
         query = jnp.where(own_block, jnp.concatenate([query] * 4, axis=0), 0.0).astype(BF16)
         score = lax.dot_general(keys[:, aligned(g, 256)], query, NT, preferred_element_type=F32) * factor
         most = jnp.max(score, axis=0, keepdims=True)
@@ -487,18 +493,21 @@
         s_g[2 * g + 1, pl.ds(32, 8), :] = jnp.where(left[0:8], turned_stat, stat).astype(BF16)
 
     own_group = lax.div(chip, 2)
-    offsets = sorted(range(groups), key=lambda k: -min(k % 4, 4 - k % 4) if k else 1)
+    other_chip = chip + 1 - 2 * lax.rem(chip, 2)
+    offsets = sorted(range(groups), key=lambda k: (min(k % 4, 4 - k % 4), k))
     waiting = []
     for first_at in range(0, groups, AT_ONCE):
-        now = offsets[first_at : first_at + AT_ONCE]
-        for offset in now:
-            remember(lax.rem(own_group + offset, groups))
+        now = [(offset, lax.rem(own_group + offset, groups)) for offset in offsets[first_at : first_at + AT_ONCE]]
+        for offset, g in now:
+            for other in [2 * g, 2 * g + 1] if offset else [other_chip]:
+                arrived(other)
         for target in waiting:
             deliver(target)
+        for offset, g in now:
+            remember(g)
         waiting = []
-        for offset in now:
-            g = lax.rem(own_group + offset, groups)
-            waiting += [2 * g, 2 * g + 1] if offset else [chip + 1 - 2 * lax.rem(chip, 2)]
+        for offset, g in now:
+            waiting += [2 * g, 2 * g + 1] if offset else [other_chip]
     for target in waiting:
         deliver(target)
     r_g[chip] = s_g[chip]
@@ -589,13 +598,13 @@
             v(chips, rows, LANES), v(chips, rows, LANES),
             v(rows, LANES), v(rows, 2 * LANES),
             v(chips, rows, LANES), v(chips, rows, LANES),
-            v(rows + 8, LANES), v(chips, rows + 8, LANES),
+            v(rows, LANES), v(chips, rows, LANES),
             v(chips, 40, LANES), v(chips, 40, LANES),
             v(rows, LANES), v(chips, rows, LANES),
-            f(rows, 4 * LANES), f(rows, 4 * LANES), f(rows, LANES), f(rows, LANES),
+            f(rows, 4 * LANES), f(rows, 4 * LANES), f(rows, LANES), f(rows, LANES), v(8, LANES), v(chips, 8, LANES),
             sems(15), sems(13), sems(13),
             sems(chips), sems(chips), sems(nb), sems(nb), sems(nb), sems(nb), sems(chips), sems(chips),
-            sems(chips), sems(chips), sems(chips), sems(chips), sems(chips), sems(chips), sems(chips), sems(chips),
+            sems(chips), sems(chips), sems(chips), sems(chips), sems(chips), sems(chips), sems(chips), sems(chips), sems(chips), sems(chips),
         ],
         compiler_params=pltpu.CompilerParams(
             collective_id=0, has_side_effects=True, vmem_limit_bytes=VMEM_BYTES

time: 67.8 us -> 68.8 us (1.015)
  Pallas kernels: 67.1 us -> 68 us
    pallas_call x1, Pallas kernels: 67.1 us -> 68 us  [body(): pl.pallas_call(functools.partial(kernel, nb, nc, d_model), out_shape=pltp...]
where the time goes in v6:
time: 68.8 us; the launch traced here: 68.6 us
  Pallas kernels  68 us (99%)
    pallas_call x1, Pallas kernels, body(): pl.pallas_call(functools.partial(kernel, nb, nc, d_model), out_shape=pltp...  68 us

profile of v6, /device:TPU:1, one launch (start us, length us, event | category | flops | bytes accessed | tf_op | source)
XLA Modules:
  0.0 68.6 jit_solution(8949847465875894547)
XLA Ops:
  0.0 68.0 %shard_map.109 = bf16[32,128]{1,0:T(8,128)(2,1)S(1)} custom-call(bf16[32,128]{1,0:T(8,128)(2,1)} %hid_hbm.1, bf16[1,128]{1,0:T(2,128)(2,1)} %bitcast.10, bf16[1,128]{1,0:T(2,128)(2,1)} %bitcast.11, s32[1,256]{1,0:T(1,128)} %bitcast.8, s32[1,256]{1,0:T(1,128)} %bitcast.9, bf16[3,4096,128]{2,1,0:T(8,128)(2,1)} %bitcast.6, bf16[128,4096]{1,0:T(8,128)(2,1)} %wso_hbm.1, ...), custom_call_target="tpu_custom_call" | custom-call | tf_op jit(solution)/shard_map/pallas_call | solution.py:584
  68.0 0.6 copy.13

commit v7 on v5

--- a/solution.py
+++ b/solution.py
@@ -14,7 +14,7 @@
 EPS = 1e-06
 LANES = 128
 VMEM_BYTES = 64000000
-AT_ONCE = 2
+AT_ONCE = 4
 
 
 def aligned(block, size=LANES):
@@ -70,6 +70,7 @@
         return (k + 2) % half
 
     steps = sorted(range(1, half), key=lambda k: -hops(k))
+    beam_steps = sorted(range(1, nb), key=lambda k: -min(k % 4, 4 - k % 4))
     far = sorted(slot(k) for k in range(half) if hops(k) >= 3)
     near = [at for at in range(half) if at not in far]
 
@@ -83,7 +84,8 @@
         pl.semaphore_signal(barrier, inc=1, device_id=(lax.rem(b + k, nb), c), device_id_type=MESH)
         return carry
 
-    lax.fori_loop(1, half, greet_blk, 0)
+    for k in steps:
+        greet_blk(k, 0)
     lax.fori_loop(1, nb, greet_beam, 0)
     pl.semaphore_signal(barrier, inc=1, device_id=(b, partner), device_id_type=MESH)
 
@@ -139,7 +141,6 @@
             pltpu.make_async_copy(block(g, core), place_at(at_slot, g, core), load_sem.at[6 + at]).start()
         return carry
 
-    lax.fori_loop(0, half, keep, 0)
 
     def remote(src, dst, send, recv, where):
         return pltpu.make_async_remote_copy(
@@ -211,16 +212,12 @@
                 ).start()
 
     def scatter_products(products, src, dst, send, recv):
-        before = None
         for which in (far, near):
             if which:
                 terms = products(which)
                 for at, which_slot in enumerate(which):
                     src[which_slot] = terms[:, at * LANES : at * LANES + LANES].astype(BF16)
-                if before:
-                    scatter_send(src, dst, send, recv, before)
-                before = which
-        scatter_send(src, dst, send, recv, before)
+                scatter_send(src, dst, send, recv, which)
         drains.append(functools.partial(simple_drain, src.at[0], send))
 
     def taken_columns(ref, rows_at, which):
@@ -253,6 +250,7 @@
     pl.semaphore_wait(barrier, half + nb - 1)
     gather_start(s_a, g_a, a_send, a_recv)
     pair_start(s_x, g_x.at[:, aligned(core)], 8)
+    lax.fori_loop(0, half, keep, 0)
     swap_start(0, 1, 2)
 
     ready(5)
@@ -311,7 +309,8 @@
         remote(s_c, my_queries, c_send.at[k], c_recv.at[b], (lax.rem(b + k, nb), c)).start()
         return carry
 
-    lax.fori_loop(1, nb, send_c, 0)
+    for k in beam_steps:
+        send_c(k, 0)
 
     def drain_c():
         def step(k, carry):
@@ -372,7 +371,8 @@
         remote(s_d.at[aligned(target, rows), :], r_d.at[b], d_send.at[k], d_recv.at[b], (target, c)).start()
         return carry
 
-    lax.fori_loop(1, nb, send_d, 0)
+    for k in beam_steps:
+        send_d(k, 0)
 
     def drain_d():
         def step(k, carry):
@@ -488,19 +488,13 @@
 
     own_group = lax.div(chip, 2)
     offsets = sorted(range(groups), key=lambda k: -min(k % 4, 4 - k % 4) if k else 1)
-    waiting = []
     for first_at in range(0, groups, AT_ONCE):
-        now = offsets[first_at : first_at + AT_ONCE]
-        for offset in now:
-            remember(lax.rem(own_group + offset, groups))
-        for target in waiting:
-            deliver(target)
-        waiting = []
-        for offset in now:
-            g = lax.rem(own_group + offset, groups)
-            waiting += [2 * g, 2 * g + 1] if offset else [chip + 1 - 2 * lax.rem(chip, 2)]
-    for target in waiting:
-        deliver(target)
+        now = [(offset, lax.rem(own_group + offset, groups)) for offset in offsets[first_at : first_at + AT_ONCE]]
+        for offset, g in now:
+            remember(g)
+        for offset, g in now:
+            for target in [2 * g, 2 * g + 1] if offset else [chip + 1 - 2 * lax.rem(chip, 2)]:
+                deliver(target)
     r_g[chip] = s_g[chip]
 
     def drain_g():
@@ -527,7 +521,11 @@
 
     s_h[...] = crossed
     g_h[slot(0)] = crossed
+    earlier = list(drains)
+    drains.clear()
     gather_start(s_h, g_h, h_send, h_recv)
+    for drain in earlier:
+        drain()
 
     def products(which, who):
         block = jnp.concatenate([g_h[at] for at in which], axis=1)

time: 67.8 us -> 66.9 us (0.987)
  Pallas kernels: 67.1 us -> 66.1 us
    pallas_call x1, Pallas kernels: 67.1 us -> 66.1 us  [body(): pl.pallas_call(functools.partial(kernel, nb, nc, d_model), out_shape=pltp...]
where the time goes in v7:
time: 66.9 us; the launch traced here: 66.7 us
  Pallas kernels  66.1 us (99%)
    pallas_call x1, Pallas kernels, body(): pl.pallas_call(functools.partial(kernel, nb, nc, d_model), out_shape=pltp...  66.1 us

profile of v7, /device:TPU:1, one launch (start us, length us, event | category | flops | bytes accessed | tf_op | source)
XLA Modules:
  0.0 66.7 jit_solution(4278002895745493081)
XLA Ops:
  0.0 66.1 %shard_map.109 = bf16[32,128]{1,0:T(8,128)(2,1)S(1)} custom-call(bf16[32,128]{1,0:T(8,128)(2,1)} %hid_hbm.1, bf16[1,128]{1,0:T(2,128)(2,1)} %bitcast.10, bf16[1,128]{1,0:T(2,128)(2,1)} %bitcast.11, s32[1,256]{1,0:T(1,128)} %bitcast.8, s32[1,256]{1,0:T(1,128)} %bitcast.9, bf16[3,4096,128]{2,1,0:T(8,128)(2,1)} %bitcast.6, bf16[128,4096]{1,0:T(8,128)(2,1)} %wso_hbm.1, ...), custom_call_target="tpu_custom_call" | custom-call | tf_op jit(solution)/shard_map/pallas_call | solution.py:573
  66.1 0.6 copy.13

commit v8 on v7

--- a/solution.py
+++ b/solution.py
@@ -84,9 +84,12 @@
         pl.semaphore_signal(barrier, inc=1, device_id=(lax.rem(b + k, nb), c), device_id_type=MESH)
         return carry
 
-    for k in steps:
+    for k in steps[: half // 2]:
         greet_blk(k, 0)
-    lax.fori_loop(1, nb, greet_beam, 0)
+    for k in beam_steps:
+        greet_beam(k, 0)
+    for k in steps[half // 2 :]:
+        greet_blk(k, 0)
     pl.semaphore_signal(barrier, inc=1, device_id=(b, partner), device_id_type=MESH)
 
     loads = [

time: 66.9 us -> 66.9 us (level)
  no operation moved by 1% of the time
where the time goes in v8:
time: 66.9 us; the launch traced here: 66.8 us
  Pallas kernels  66.2 us (99%)
    pallas_call x1, Pallas kernels, body(): pl.pallas_call(functools.partial(kernel, nb, nc, d_model), out_shape=pltp...  66.2 us

profile of v8, /device:TPU:1, one launch (start us, length us, event | category | flops | bytes accessed | tf_op | source)
XLA Modules:
  0.0 66.8 jit_solution(14236438987250140042)
XLA Ops:
  0.0 66.2 %shard_map.109 = bf16[32,128]{1,0:T(8,128)(2,1)S(1)} custom-call(bf16[32,128]{1,0:T(8,128)(2,1)} %hid_hbm.1, bf16[1,128]{1,0:T(2,128)(2,1)} %bitcast.10, bf16[1,128]{1,0:T(2,128)(2,1)} %bitcast.11, s32[1,256]{1,0:T(1,128)} %bitcast.8, s32[1,256]{1,0:T(1,128)} %bitcast.9, bf16[3,4096,128]{2,1,0:T(8,128)(2,1)} %bitcast.6, bf16[128,4096]{1,0:T(8,128)(2,1)} %wso_hbm.1, ...), custom_call_target="tpu_custom_call" | custom-call | tf_op jit(solution)/shard_map/pallas_call | solution.py:576
  66.2 0.6 copy.13
